TPU v7x, 768 devices: a whole 4x8x12 slice. The times are simulated.
768 devices in a mesh: frame: 48 (over x, z_lo, core), space: 16 (over z_hi, y).
Axes of the slice: x: 4, y: 8, z: 12 (z_hi: 2, z_lo: 6; z = z_hi * 6 + z_lo), core: 2. Of those that a mesh axis runs over, the one named last changes fastest.
Arguments:
- residual_in: bfloat16 [96, 1536, 1152], P('frame', 'space'), may hold values from -40 to 40
- q_spatial: bfloat16 [96, 1536, 1152], P('frame', 'space'), may hold values from -400 to 400
- k_spatial: bfloat16 [96, 1536, 1152], P('frame', 'space'), may hold values from -12 to 12
- v_spatial: bfloat16 [96, 1536, 1152], P('frame', 'space'), may hold values from -24 to 24
- w_out: bfloat16 [1152, 1152], replicated, may hold values from -0.1875 to 0.1875
- modulation: float32 [3, 1152], replicated, may hold values from -3 to 3
- w_temporal: bfloat16 [1152, 1728], replicated, may hold values from -4 to 4
Outputs:
- residual_out: bfloat16 [96, 1536, 1152], P('frame', 'space')
- temporal_mix: bfloat16 [96, 1536, 576], P('frame', 'space')
All inputs are finite; a program needn't handle non-finite values.
Results may differ from a plain program's by a relative error of at most 0.0085.
Values may be sent and summed in bfloat16 or wider, within the bound.
A program may use at most 32 MiB of HBM per device.

v0:
```python
import math

import jax
import jax.numpy as jnp
from jax import lax
from jax.sharding import PartitionSpec as P

HEAD_DIM = 72
T_HEADS = 8


def attend_block(queries, keys_in, values_in, head_count):
    lengths = queries.shape[0]
    columns = queries.shape[1]
    head_size = columns // head_count
    query_heads = queries.reshape(lengths, head_count, head_size)
    key_heads = keys_in.reshape(keys_in.shape[0], head_count, head_size)
    value_heads = values_in.reshape(values_in.shape[0], head_count, head_size)
    scores = jnp.einsum(
        "qha,kha->hqk", query_heads, key_heads, preferred_element_type=jnp.float32
    ) / math.sqrt(head_size)
    largest = jnp.max(scores, axis=-1, keepdims=True)
    expons = jnp.exp(scores - largest)
    totals = jnp.sum(expons, axis=-1, keepdims=True)
    rounded = expons.astype(jnp.bfloat16)
    mixed = (
        jnp.einsum("hqk,kha->hqa", rounded, value_heads, preferred_element_type=jnp.float32)
        / totals
    )
    return jnp.transpose(mixed, (1, 0, 2)).reshape(lengths, columns).astype(jnp.bfloat16)


def frame_attend(queries, keys_in, values_in, head_count):
    lengths, columns = queries.shape
    block = math.gcd(lengths, 512)
    grouped = queries.reshape(lengths // block, block, columns)
    outcome = lax.map(
        lambda query_block: attend_block(query_block, keys_in, values_in, head_count), grouped
    )
    return outcome.reshape(lengths, columns)


def spatial_heads_attend(triple):
    queries, keys_in, values_in = triple
    head_count = queries.shape[2] // HEAD_DIM
    return lax.map(
        lambda framed: frame_attend(framed[0], framed[1], framed[2], head_count),
        (queries, keys_in, values_in),
    )


def temporal_attend(grouped_rows, head_count):
    frame_count, group_count, place_count, triple_width = grouped_rows.shape
    inner = triple_width // 3
    head_size = inner // head_count
    places = group_count * place_count
    shaped = grouped_rows.reshape(frame_count, places, 3, head_count, head_size)
    queries = shaped[:, :, 0]
    keys_in = shaped[:, :, 1]
    values_in = shaped[:, :, 2]
    scores = jnp.einsum(
        "fpha,gpha->phfg", queries, keys_in, preferred_element_type=jnp.float32
    ) / math.sqrt(head_size)
    largest = jnp.max(scores, axis=-1, keepdims=True)
    expons = jnp.exp(scores - largest)
    totals = jnp.sum(expons, axis=-1, keepdims=True)
    rounded = expons.astype(jnp.bfloat16)
    mixed = (
        jnp.einsum("phfg,gpha->phfa", rounded, values_in, preferred_element_type=jnp.float32)
        / totals
    )
    mixed = jnp.transpose(mixed, (2, 0, 1, 3)).reshape(frame_count, group_count, place_count, inner)
    return mixed.astype(jnp.bfloat16)


def modulate(residual_out, modulation):
    values32 = residual_out.astype(jnp.float32)
    center = jnp.mean(values32, axis=-1, keepdims=True)
    spread = jnp.mean((values32 - center) ** 2, axis=-1, keepdims=True)
    normed = (values32 - center) * lax.rsqrt(spread + 1e-06) * (1.0 + modulation[1]) + modulation[0]
    return normed.astype(jnp.bfloat16)


def per_device(residual_in, q_spatial, k_spatial, v_spatial, w_out, modulation, w_temporal):
    frame_count, place_count, features = residual_in.shape
    groups = lax.axis_size("frame")
    per_group = place_count // groups
    head_mix = spatial_heads_attend(
        (
            lax.all_to_all(q_spatial, "space", split_axis=2, concat_axis=1, tiled=True),
            lax.all_to_all(k_spatial, "space", split_axis=2, concat_axis=1, tiled=True),
            lax.all_to_all(v_spatial, "space", split_axis=2, concat_axis=1, tiled=True),
        )
    )
    spatial_mix = lax.all_to_all(head_mix, "space", split_axis=1, concat_axis=2, tiled=True)
    branch = jnp.dot(
        spatial_mix.reshape(frame_count * place_count, features),
        w_out,
        preferred_element_type=jnp.float32,
    )
    branch = branch.reshape(frame_count, place_count, features)
    residual_out = (residual_in.astype(jnp.float32) + modulation[2] * branch).astype(jnp.bfloat16)
    normed = modulate(residual_out, modulation)
    projected = jnp.dot(
        normed.reshape(frame_count * place_count, features),
        w_temporal,
        preferred_element_type=jnp.float32,
    )
    projected = projected.astype(jnp.bfloat16).reshape(
        frame_count, groups, per_group, w_temporal.shape[1]
    )
    mixed = temporal_attend(
        lax.all_to_all(projected, "frame", split_axis=1, concat_axis=0, tiled=True), T_HEADS
    )
    returned = lax.all_to_all(mixed, "frame", split_axis=0, concat_axis=1, tiled=True)
    temporal_mix = returned.reshape(frame_count, place_count, returned.shape[3])
    return (residual_out, temporal_mix)


def solution(mesh):
    return jax.shard_map(
        per_device,
        mesh=mesh,
        in_specs=(
            P("frame", "space", None),
            P("frame", "space", None),
            P("frame", "space", None),
            P("frame", "space", None),
            P(),
            P(),
            P(),
        ),
        out_specs=(P("frame", "space", None), P("frame", "space", None)),
        check_vma=False,
    )
```

profile of v0, /device:TPU:1, one launch (start us, length us, event | category | flops | bytes accessed | tf_op | source)
XLA Modules:
  0.0 270.7 jit_solution(11564291711948528898)
XLA Ops:
  0.6 2.2 copy.49
  2.9 20.4 %all-to-all-start = ((bf16[2,96,1152]{1,0,2:T(2,128)(2,1)}), bf16[2,96,1152]{1,0,2:T(2,128)(2,1)S(1)}, u32[]{:S(2)}, u32[]{:S(2)}) async-start(bf16[2,96,1152]{1,0,2:T(2,128)(2,1)} %copy.49), calls=%async_computation | async-start | bytes 1179648 | tf_op jit(solution)/shard_map/all_to_all | solution.py:90
  23.3 2.1 copy.52
  25.4 15.6 %all-to-all-done = bf16[2,96,1152]{1,0,2:T(2,128)(2,1)S(1)} async-done(((bf16[2,96,1152]{1,0,2:T(2,128)(2,1)}), bf16[2,96,1152]{1,0,2:T(2,128)(2,1)S(1)}, u32[]{:S(2)}, u32[]{:S(2)}) %all-to-all-start) | async-done | bytes 442400 | tf_op jit(solution)/shard_map/all_to_all | solution.py:90
  41.0 10.5 %all-to-all-start.1 = ((bf16[2,96,1152]{1,0,2:T(2,128)(2,1)}), bf16[2,96,1152]{1,0,2:T(2,128)(2,1)}, u32[]{:S(2)}, u32[]{:S(2)}) async-start(bf16[2,96,1152]{1,0,2:T(2,128)(2,1)} %copy.52), calls=%async_computation.1 | async-start | bytes 1179648 | tf_op jit(solution)/shard_map/all_to_all | solution.py:91
  51.5 2.1 copy.55
  53.6 15.5 %all-to-all-done.1 = bf16[2,96,1152]{1,0,2:T(2,128)(2,1)} async-done(((bf16[2,96,1152]{1,0,2:T(2,128)(2,1)}), bf16[2,96,1152]{1,0,2:T(2,128)(2,1)}, u32[]{:S(2)}, u32[]{:S(2)}) %all-to-all-start.1) | async-done | bytes 442400 | tf_op jit(solution)/shard_map/all_to_all | solution.py:91
  69.1 10.9 %all-to-all-start.2 = ((bf16[2,96,1152]{1,0,2:T(2,128)(2,1)}), bf16[2,96,1152]{1,0,2:T(2,128)(2,1)}, u32[]{:S(2)}, u32[]{:S(2)}) async-start(bf16[2,96,1152]{1,0,2:T(2,128)(2,1)} %copy.55), calls=%async_computation.2 | async-start | bytes 1179648 | tf_op jit(solution)/shard_map/all_to_all | solution.py:92
  80.9 2.2 copy.74
  84.3 1.2 copy.75
  85.5 12.1 %all-to-all-done.2 = bf16[2,96,1152]{1,0,2:T(2,128)(2,1)} async-done(((bf16[2,96,1152]{1,0,2:T(2,128)(2,1)}), bf16[2,96,1152]{1,0,2:T(2,128)(2,1)}, u32[]{:S(2)}, u32[]{:S(2)}) %all-to-all-start.2) | async-done | bytes 442400 | tf_op jit(solution)/shard_map/all_to_all | solution.py:92
  97.6 1.1 copy.56
  98.7 1.2 copy.76
  99.9 30.8 %while.21 = (s32[]{:T(128)}, bf16[2,1536,72]{2,1,0:T(8,128)(2,1)}, bf16[2,1536,72]{2,1,0:T(8,128)(2,1)}, bf16[2,1536,72]{2,1,0:T(8,128)(2,1)}, bf16[2,1536,72]{2...) while((s32[]{:T(128)}, bf16[2,1536,72]{2,1,0:T(8,128)(2,1)}, bf16[2,1536,72]{2,1,0:T(8,128)(2,1)}, ...), condition=%wide.region_5.6_spmd, body=%wide.region_0.5_spmd.sunk | while | flops 231283712 | bytes 12478710 | solution.py:46
  99.9 1.8 constant_dynamic-slice_fusion.2
  101.7 1.2 dynamic-slice_bitcast_fusion.3
  102.9 10.5 %while.22 = (s32[]{:T(128)}, bf16[3,512,72]{1,2,0:T(8,128)(2,1)}, bf16[3,512,72]{2,1,0:T(8,128)(2,1)}, bf16[1536,72]{1,0:T(8,128)(2,1)S(1)}, bf16[1536,72]{1,0:T(8,128)(2,1)S(1)}, /*index=5*/s32[]{:T(128)}) while((s32[]{:T(128)}, bf16[3,512,72]{1,2,0:T(8,128)(2,1)}, bf16[3,512,72]{2,1,0:T(8,128)(2,1)}, bf16[1536,72]{1,0:T(8,128)(2,1)S(1)}, ...), condition=%wide.region_4.4_spmd, body=%wide.region_1.3_spmd.sunk | while | flops 231283712 | bytes 10094677 | solution.py:37
  102.9 1.6 fusion.57
  105.0 1.4 fusion.59
  106.4 1.6 fusion.57
  108.5 1.4 fusion.59
  109.9 1.6 fusion.57
  112.0 1.4 fusion.59
  113.4 1.2 copy.84
  115.3 1.8 constant_dynamic-slice_fusion.2
  117.1 1.2 dynamic-slice_bitcast_fusion.3
  118.2 10.5 %while.22 = (s32[]{:T(128)}, bf16[3,512,72]{1,2,0:T(8,128)(2,1)}, bf16[3,512,72]{2,1,0:T(8,128)(2,1)}, bf16[1536,72]{1,0:T(8,128)(2,1)S(1)}, bf16[1536,72]{1,0:T(8,128)(2,1)S(1)}, /*index=5*/s32[]{:T(128)}) while((s32[]{:T(128)}, bf16[3,512,72]{1,2,0:T(8,128)(2,1)}, bf16[3,512,72]{2,1,0:T(8,128)(2,1)}, bf16[1536,72]{1,0:T(8,128)(2,1)S(1)}, ...), condition=%wide.region_4.4_spmd, body=%wide.region_1.3_spmd.sunk | while | flops 231283712 | bytes 10094677 | solution.py:37
  118.2 1.6 fusion.57
  120.4 1.4 fusion.59
  121.7 1.6 fusion.57
  123.9 1.4 fusion.59
  125.2 1.6 fusion.57
  127.4 1.4 fusion.59
  128.7 1.2 copy.84
  130.7 7.5 %copy.61 = bf16[2,1536,72]{2,0,1:T(2,128)(2,1)} copy(bf16[2,1536,72]{2,1,0:T(8,128)(2,1)} %get-tuple-element.56) | data formatting | bytes 884736 | tf_op jit(solution)/shard_map/while | solution.py:46
  138.1 11.0 %all-to-all-start.3 = ((bf16[2,1536,72]{2,0,1:T(2,128)(2,1)}), bf16[2,1536,72]{2,0,1:T(2,128)(2,1)S(1)}, u32[]{:S(2)}, u32[]{:S(2)}) async-start(bf16[2,1536,72]{2,0,1:T(2,128)(2,1)} %copy.61), calls=%async_computation.3 | async-start | bytes 1572864 | tf_op jit(solution)/shard_map/all_to_all | solution.py:95
  149.2 19.5 %all-to-all-done.3 = bf16[2,1536,72]{2,0,1:T(2,128)(2,1)S(1)} async-done(((bf16[2,1536,72]{2,0,1:T(2,128)(2,1)}), bf16[2,1536,72]{2,0,1:T(2,128)(2,1)S(1)}, u32[]{:S(2)}, u32[]{:S(2)}) %all-to-all-start.3) | async-done | bytes 442400 | tf_op jit(solution)/shard_map/all_to_all | solution.py:95
  168.7 1.8 copy.62
  170.5 2.3 convert_reduce_fusion
  173.5 2.2 convolution_convert_fusion
  175.7 2.7 reshape.99
  178.4 1.6 copy.64
  180.0 58.0 %all_to_all.99 = bf16[2,48,2,1728]{3,2,0,1:T(2,128)(2,1)S(1)} all-to-all(bf16[2,48,2,1728]{3,2,0,1:T(2,128)(2,1)S(1)} %copy.64), channel_id=1, replica_groups=mesh['frame'=48,'space'=16] {'frame'}, dimensions={1} | all-to-all | bytes 1327104 | tf_op jit(solution)/shard_map/all_to_all | solution.py:113
  238.0 3.0 %reshape.100 = bf16[96,2,3,8,72]{4,3,2,1,0:T(8,128)(2,1)} reshape(bf16[48,2,1,2,1728]{4,3,1,0,2:T(2,128)(2,1)S(1)} %bitcast.96) | data formatting | bytes 1327104 | tf_op jit(solution)/shard_map/reshape | solution.py:57
  241.0 2.2 fusion.41
  243.2 2.0 copy.81
  246.7 1.4 fusion.42
  248.8 21.1 %all_to_all.100 = bf16[96,1,2,576]{3,2,1,0:T(2,128)(2,1)S(1)} all-to-all(bf16[96,1,2,576]{3,2,1,0:T(2,128)(2,1)S(1)} %copy.69), channel_id=1, replica_groups=mesh['frame'=48,'space'=16] {'frame'}, dimensions={0} | all-to-all | bytes 442368 | tf_op jit(solution)/shard_map/all_to_all | solution.py:115
  (33 shorter events, 10.8 us)
Async XLA Ops:
  0.6 169.9 %copy-start = (bf16[1152,1152]{1,0:T(8,128)(2,1)S(1)}, bf16[1152,1152]{1,0:T(8,128)(2,1)}, u32[]{:S(2)}) copy-start(bf16[1152,1152]{1,0:T(8,128)(2,1)} %param.15) | copy-start | bytes 7962628
  2.9 38.2 %all-to-all-start = ((bf16[2,96,1152]{1,0,2:T(2,128)(2,1)}), bf16[2,96,1152]{1,0,2:T(2,128)(2,1)S(1)}, u32[]{:S(2)}, u32[]{:S(2)}) async-start(bf16[2,96,1152]{1,0,2:T(2,128)(2,1)} %copy.49), calls=%async_computation | async-start | bytes 1179648 | tf_op jit(solution)/shard_map/all_to_all | solution.py:90
  41.0 28.1 %all-to-all-start.1 = ((bf16[2,96,1152]{1,0,2:T(2,128)(2,1)}), bf16[2,96,1152]{1,0,2:T(2,128)(2,1)}, u32[]{:S(2)}, u32[]{:S(2)}) async-start(bf16[2,96,1152]{1,0,2:T(2,128)(2,1)} %copy.52), calls=%async_computation.1 | async-start | bytes 1179648 | tf_op jit(solution)/shard_map/all_to_all | solution.py:91
  69.1 28.5 %all-to-all-start.2 = ((bf16[2,96,1152]{1,0,2:T(2,128)(2,1)}), bf16[2,96,1152]{1,0,2:T(2,128)(2,1)}, u32[]{:S(2)}, u32[]{:S(2)}) async-start(bf16[2,96,1152]{1,0,2:T(2,128)(2,1)} %copy.55), calls=%async_computation.2 | async-start | bytes 1179648 | tf_op jit(solution)/shard_map/all_to_all | solution.py:92
  130.7 18.4 %copy-start.2 = (f32[3,1152]{1,0:T(4,128)S(1)}, f32[3,1152]{1,0:T(4,128)}, u32[]{:S(2)}) copy-start(f32[3,1152]{1,0:T(4,128)} %param.16) | copy-start | bytes 41476
  138.1 30.6 %all-to-all-start.3 = ((bf16[2,1536,72]{2,0,1:T(2,128)(2,1)}), bf16[2,1536,72]{2,0,1:T(2,128)(2,1)S(1)}, u32[]{:S(2)}, u32[]{:S(2)}) async-start(bf16[2,1536,72]{2,0,1:T(2,128)(2,1)} %copy.61), calls=%async_computation.3 | async-start | bytes 1572864 | tf_op jit(solution)/shard_map/all_to_all | solution.py:95
  170.5 3.0 %copy-start.3 = (bf16[1152,1728]{0,1:T(8,128)(2,1)S(1)}, bf16[1152,1728]{0,1:T(8,128)(2,1)}, u32[]{:S(2)}) copy-start(bf16[1152,1728]{0,1:T(8,128)(2,1)} %param.17) | copy-start | bytes 11943940
  172.8 2.9 %copy-start.1 = (bf16[2,96,1152]{2,1,0:T(8,128)(2,1)}, bf16[2,96,1152]{2,1,0:T(8,128)(2,1)S(1)}, u32[]{:S(2)}) copy-start(bf16[2,96,1152]{2,1,0:T(8,128)(2,1)S(1)} %get-tuple-element.102) | copy-start | bytes 1327108
where the time goes:
time: 272 us; the launch traced here: 271 us
  blocking collectives  79.1 us (29%)
  waiting for transfers between devices  62.8 us (23%)
  starting transfers between devices  52.7 us (19%)
  local copies, waits for them, and re-layouts  47.4 us (17%)
  matrix products  23.7 us (9%)
  other arithmetic  4.26 us (2%)
    all_to_all x1, blocking collectives, per_device(): lax.all_to_all(projected, 'frame', split_axis=1, concat_axis=0, tiled=True)  58 us
    all_to_all x1, blocking collectives, per_device(): lax.all_to_all(mixed, 'frame', split_axis=0, concat_axis=1, tiled=True)  21.1 us
    all_to_all x1, starting transfers between devices, per_device(): lax.all_to_all(q_spatial, 'space', split_axis=2, concat_axis=1, tiled=True)  20.4 us
    all_to_all x1, waiting for transfers between devices, per_device(): lax.all_to_all(head_mix, 'space', split_axis=1, concat_axis=2, tiled=True)  19.5 us
    all_to_all x1, waiting for transfers between devices, per_device(): lax.all_to_all(q_spatial, 'space', split_axis=2, concat_axis=1, tiled=True)  15.6 us
    all_to_all x1, waiting for transfers between devices, per_device(): lax.all_to_all(k_spatial, 'space', split_axis=2, concat_axis=1, tiled=True)  15.5 us
    while x4, local copies, waits for them, and re-layouts, spatial_heads_attend(): lax.map(lambda framed: frame_attend(framed[0], framed[1], framed[2], head...  12.1 us
    all_to_all x1, waiting for transfers between devices, per_device(): lax.all_to_all(v_spatial, 'space', split_axis=2, concat_axis=1, tiled=True)  12.1 us
  transfers between devices with their start and end apart: 4, of which 4 were waited for; matrix products, arithmetic and copies ran while one was open for 4% of the time, Pallas kernels for 0%

commit v1 on v0

v1 whole, which is shorter than its diff:
```python
import functools
import math

import jax
import jax.numpy as jnp
from jax import lax
from jax.experimental import pallas as pl
from jax.experimental.pallas import tpu as pltpu
from jax.sharding import PartitionSpec as P

MESH = pl.DeviceIdType.MESH
HEAD = 72
T_HEADS = 8
BF = jnp.bfloat16
F32 = jnp.float32
EXP2_SCALE = math.log2(math.e) / math.sqrt(HEAD)


def lane_iota(rows):
    return lax.broadcasted_iota(jnp.int32, (rows, 128), 1)


def roll_lanes(x, shift):
    shift = shift % 128
    if shift == 0:
        return x
    return pltpu.roll(x, shift, axis=1)


def send(src, dst, ssem, rsem, device):
    return pltpu.make_async_remote_copy(
        src_ref=src, dst_ref=dst, send_sem=ssem, recv_sem=rsem, device_id=device, device_id_type=MESH
    )


def spatial_kernel(
    q_ref, k_ref, v_ref, out_ref,
    sbk, sbq, sbv, zrk, zrq, zrv, fk, fq, fv, qs, k0, k1, vs, pr, ob, zro,
    zs, zr, ys, yr, zos, zor, yos, yor,
):
    f = lax.axis_index("frame")
    s = lax.axis_index("space")
    a = s // 8
    y = lax.rem(s, 8)
    far = 1 - a
    partner = (f, far * 8 + y)
    places = q_ref.shape[1]
    half = places // 2

    barrier = pltpu.get_barrier_semaphore()
    pl.semaphore_signal(barrier, inc=1, device_id=partner, device_id_type=MESH)

    def greet(j, carry):
        pl.semaphore_signal(
            barrier, inc=1, device_id=(f, a * 8 + lax.rem(y + j, 8)), device_id_type=MESH
        )
        return carry

    lax.fori_loop(1, 8, greet, 0)

    lanes = lane_iota(places)
    half_lanes = lane_iota(half)

    def tile(ref, fr, index):
        return ref[fr, :, 128 * index : 128 * index + 128].astype(F32)

    def main_of(ref, fr, pair):
        low = tile(ref, fr, pair)
        if pair == 0:
            return low.astype(BF)
        high = tile(ref, fr, pair + 1)
        return roll_lanes(jnp.where(lanes >= 16 * pair, low, high), -16 * pair).astype(BF)

    def pack_k(fr):
        for pair in range(8):
            sbk[fr, pair, 0:places] = main_of(k_ref, fr, pair)
            left = jnp.where(
                lanes < 16,
                roll_lanes(tile(k_ref, fr, pair + 1), -16 * pair),
                jnp.where(
                    lanes < 32,
                    roll_lanes(tile(q_ref, fr, pair + 1), 16 - 16 * pair),
                    roll_lanes(tile(v_ref, fr, pair + 1), 32 - 16 * pair),
                ),
            )
            joined = jnp.where(half_lanes < 64, left[0:half], roll_lanes(left[half:places], 64))
            sbk[fr, pair, places : places + half] = joined.astype(BF)

    def pack(ref, buf, fr):
        for pair in range(8):
            buf[fr, pair] = main_of(ref, fr, pair)

    sent = ((sbk, zrk, fk), (sbq, zrq, fq), (sbv, zrv, fv))

    def z_copy(t, j):
        buf, relay, final = sent[t]
        target = lax.rem(y + j, 8)
        return send(buf.at[far, target], relay.at[j], zs.at[t, j], zr.at[t, j], partner)

    def z_home(t):
        buf, relay, final = sent[t]
        return send(buf.at[far, y], final.at[s], zs.at[t, 0], zr.at[t, 0], partner)

    def y_copy(t, j):
        buf, relay, final = sent[t]
        target = lax.rem(y + j, 8)
        return send(
            buf.at[a, target], final.at[s], ys.at[0, t, j], yr.at[0, t, j], (f, a * 8 + target)
        )

    def y_relay(t, j):
        buf, relay, final = sent[t]
        target = lax.rem(y + j, 8)
        return send(
            relay.at[j], final.at[far * 8 + y], ys.at[1, t, j], yr.at[1, t, j],
            (f, a * 8 + target),
        )

    def each(low, high, body):
        def step(j, carry):
            body(j)
            return carry

        lax.fori_loop(low, high, step, 0)

    pack_k(far)
    pl.semaphore_wait(barrier, 8)

    def z_start(t):
        each(1, 8, lambda j: z_copy(t, j).start())
        z_home(t).start()

    def y_start(t):
        each(1, 8, lambda j: y_copy(t, j).start())

    z_start(0)
    pack(q_ref, sbq, far)
    z_start(1)
    pack(v_ref, sbv, far)
    z_start(2)
    pack_k(a)
    y_start(0)
    pack(q_ref, sbq, a)
    y_start(1)
    pack(v_ref, sbv, a)
    y_start(2)
    fk[s] = sbk[a, y]
    fq[s] = sbq[a, y]
    fv[s] = sbv[a, y]

    def forward(t, j):
        z_copy(t, j).wait_recv()
        y_relay(t, j).start()

    def settle(t):
        z_home(t).wait_recv()
        each(1, 8, lambda j: y_copy(t, j).wait_recv())
        each(1, 8, lambda j: y_relay(t, j).wait_recv())

    each(1, 8, lambda j: forward(0, j))
    each(1, 8, lambda j: forward(1, j))
    settle(0)
    settle(1)

    zero = jnp.zeros((places, 128), F32)

    def spread(block):
        rows = pl.ds(pl.multiple_of(block * places, places), places)
        main = fk[block, 0:places].astype(F32)
        packed = fk[block, places : places + half].astype(F32)
        left = jnp.concatenate([packed, roll_lanes(packed, 64)], axis=0)
        k0[rows, :] = jnp.where(lanes < HEAD, main, zero).astype(BF)
        k1[rows, 0:128] = jnp.where(lanes < HEAD, zero, main).astype(BF)
        k1[rows, 128:256] = jnp.where(lanes < 16, left, zero).astype(BF)
        qs[rows, 0:128] = fq[block]
        qs[rows, 128:256] = roll_lanes(left, -16).astype(BF)
        vs[rows, 128:256] = jnp.where(
            lanes < 16, roll_lanes(left, -32), jnp.where(lanes == 16, 1.0, 0.0)
        ).astype(BF)

    each(0, 16, spread)

    big = 4 * places

    def weigh(step):
        rows = pl.ds(pl.multiple_of(step * big, big), big)
        for head in range(2):
            if head == 0:
                left_side, keys = qs[rows, 0:128], k0[...]
            else:
                left_side, keys = qs[rows, :], k1[...]
            scores = lax.dot_general(
                left_side, keys, (((1,), (1,)), ((), ())), preferred_element_type=F32
            )
            largest = jnp.max(scores, axis=1, keepdims=True)
            pr[head, rows, :] = jnp.exp2((scores - largest) * EXP2_SCALE).astype(BF)
        forward(2, 2 * step + 1)

        @pl.when(step < 3)
        def _():
            forward(2, 2 * step + 2)

    each(0, 4, weigh)
    settle(2)

    def place_v(block):
        rows = pl.ds(pl.multiple_of(block * places, places), places)
        vs[rows, 0:128] = fv[block]

    each(0, 16, place_v)

    sub_lanes = lane_iota(16)

    def mix(first):
        rows = pl.ds(pl.multiple_of(first * places, places), big)
        mixed = []
        for head in range(2):
            product = jnp.dot(pr[head, rows, :], vs[...], preferred_element_type=F32)
            inverse = 1.0 / product[:, 144:145]
            mixed.append(product * inverse)
        for part in range(4):
            cut = slice(part * places, (part + 1) * places)
            ob[first + part, 0:places] = jnp.where(
                lanes < HEAD, mixed[0][cut, 0:128], mixed[1][cut, 0:128]
            ).astype(BF)
            rest = mixed[1][cut, 128:256]
            packed = rest[0:16]
            for group in range(1, 6):
                moved = roll_lanes(rest[16 * group : 16 * group + 16], 16 * group)
                packed = jnp.where(sub_lanes < 16 * group, packed, moved)
            ob[first + part, places : places + 16] = packed.astype(BF)

    def z_back(target):
        return send(
            ob.at[far * 8 + target], zro.at[target], zos.at[target], zor.at[target], partner
        )

    def z_back_home():
        return send(ob.at[far * 8 + y], out_ref.at[a, y], zos.at[y], zor.at[y], partner)

    def y_back(j):
        target = lax.rem(y + j, 8)
        return send(
            ob.at[a * 8 + target], out_ref.at[a, y], yos.at[0, j], yor.at[0, j],
            (f, a * 8 + target),
        )

    def y_back_relay(target):
        j = lax.rem(target + 8 - y, 8)
        return send(
            zro.at[target], out_ref.at[far, y], yos.at[1, j], yor.at[1, j], (f, a * 8 + target)
        )

    def z_back_start(target):
        @pl.when(target != y)
        def _():
            z_back(target).start()

        @pl.when(target == y)
        def _():
            z_back_home().start()

    def far_part(step):
        mix(far * 8 + 4 * step)
        each(4 * step, 4 * step + 4, z_back_start)

    def near_part(step):
        mix(a * 8 + 4 * step)

    each(0, 2, far_part)
    each(0, 2, near_part)
    each(1, 8, lambda j: y_back(j).start())
    out_ref[a, y] = ob[s]

    def relay_back(target):
        @pl.when(target != y)
        def _():
            z_back(target).wait_recv()
            y_back_relay(target).start()

    each(0, 8, relay_back)
    z_back_home().wait_recv()
    each(1, 8, lambda j: y_back(j).wait_recv())

    def relay_end(j):
        copy = send(
            zro.at[0], out_ref.at[far, 0], yos.at[1, j], yor.at[1, j], (f, a * 8 + lax.rem(y + j, 8))
        )
        copy.wait_recv()
        copy.wait_send()

    each(1, 8, relay_end)
    each(1, 8, lambda j: y_back(j).wait_send())

    each(0, 8, lambda target: z_back(target).wait_send())
    for t in range(3):
        z_home(t).wait_send()
        each(1, 8, lambda j: z_copy(t, j).wait_send())
        each(1, 8, lambda j: y_copy(t, j).wait_send())
        each(1, 8, lambda j: y_relay(t, j).wait_send())


def one_hot(rows_of):
    size = 192
    row = lax.broadcasted_iota(jnp.int32, (size, size), 0)
    column = lax.broadcasted_iota(jnp.int32, (size, size), 1)
    return jnp.where(column == rows_of(row), 1.0, 0.0).astype(BF)


def temporal_kernel(
    mix_ref, res_ref, wo_ref, mod_ref, wt_ref, res_out, mix_out,
    am, wp, pf, sbf, rbf, tm, sb2, rb2, fs, fr_sem, gs, gr,
):
    f = lax.axis_index("frame")
    s = lax.axis_index("space")
    n = lax.axis_size("frame")
    barrier = pltpu.get_barrier_semaphore()

    def each(low, high, body):
        def step(j, carry):
            body(j)
            return carry

        lax.fori_loop(low, high, step, 0)

    each(
        1, n,
        lambda i: pl.semaphore_signal(
            barrier, inc=1, device_id=(lax.rem(f + i, n), s), device_id_type=MESH
        ),
    )

    places = res_ref.shape[1]
    width = wt_ref.shape[1]
    inner = width // 3
    lanes16 = lane_iota(16)
    for pair in range(8):
        wp[128 * pair : 128 * pair + 128] = wo_ref[144 * pair : 144 * pair + 128]
        wp[1024 + 16 * pair : 1040 + 16 * pair] = wo_ref[144 * pair + 128 : 144 * pair + 144]
    for frame in range(2):
        base = frame * places
        for pair in range(8):
            am[base : base + places, 128 * pair : 128 * pair + 128] = mix_ref[frame, pair, 0:places]
        packs = [mix_ref[frame, pair, places : places + 16].astype(F32) for pair in range(8)]
        for group in range(6):
            joined = roll_lanes(packs[0], -16 * group)
            for pair in range(1, 8):
                moved = roll_lanes(packs[pair], 16 * pair - 16 * group)
                joined = jnp.where(lanes16 < 16 * pair, joined, moved)
            am[base + 16 * group : base + 16 * group + 16, 1024:1152] = joined.astype(BF)

    branch = jnp.dot(am[...], wp[...], preferred_element_type=F32)
    res = res_ref[...].reshape(2 * places, res_ref.shape[2]).astype(F32)
    res = (res + mod_ref[2:3, :] * branch).astype(BF)
    res_out[...] = res.reshape(res_out.shape)
    values = res.astype(F32)
    center = jnp.mean(values, axis=1, keepdims=True)
    moved = values - center
    spread = jnp.mean(moved * moved, axis=1, keepdims=True)
    normed = moved * lax.rsqrt(spread + 1e-06) * (1.0 + mod_ref[1:2, :]) + mod_ref[0:1, :]
    normed = normed.astype(BF)

    by_group = one_hot(lambda r: lax.rem(r, 2) * 96 + 2 * (r // 4) + lax.rem(r // 2, 2))
    by_place = one_hot(lambda r: 4 * (lax.rem(r, 96) // 2) + 2 * (r // 96) + lax.rem(r, 2))
    to_group = one_hot(lambda r: lax.rem(r // 2, 2) * 96 + 2 * (r // 4) + lax.rem(r, 2))
    to_rows = one_hot(lambda r: 4 * (lax.rem(r, 96) // 2) + 2 * lax.rem(r, 2) + r // 96)

    grouped = jnp.dot(by_group, normed, preferred_element_type=F32).astype(BF)
    pf[:, 1664:1792] = jnp.zeros((2 * places, 128), F32)
    pf[:, 0:width] = jnp.dot(grouped, wt_ref[...], preferred_element_type=F32)

    def eight(g):
        return pl.ds(pl.multiple_of(8 * g, 8), 8)

    def cut(g):
        both = pf[eight(g), :]
        sbf[2 * g] = both[0:4].astype(BF)
        sbf[2 * g + 1] = both[4:8].astype(BF)

    each(0, n // 2, cut)
    pl.semaphore_wait(barrier, n - 1)

    def forth(i):
        target = lax.rem(f + i, n)
        return send(sbf.at[target], rbf.at[f], fs.at[i], fr_sem.at[i], (target, s))

    each(1, n, lambda i: forth(i).start())
    rbf[f] = sbf[f]
    each(1, n, lambda i: forth(i).wait_recv())

    def gather(g):
        pf[eight(g), :] = jnp.concatenate(
            [rbf[2 * g].astype(F32), rbf[2 * g + 1].astype(F32)], axis=0
        )

    each(0, n // 2, gather)
    rows = jnp.dot(by_place, pf[...].astype(BF), preferred_element_type=F32).astype(BF)
    lanes256 = lax.broadcasted_iota(jnp.int32, (96, 256), 1)
    tm[...] = jnp.zeros(tm.shape, F32)
    for p in range(2):
        block = rows[p * 96 : p * 96 + 96]
        for head in range(T_HEADS):
            start = head * HEAD
            queries = block[:, start : start + HEAD]
            keys = block[:, inner + start : inner + start + HEAD]
            window = (start // 128) * 128
            window = min(window, 384)
            scores = lax.dot_general(
                queries, keys, (((1,), (1,)), ((), ())), preferred_element_type=F32
            )
            largest = jnp.max(scores, axis=1, keepdims=True)
            expons = jnp.exp2((scores - largest) * EXP2_SCALE)
            totals = jnp.sum(expons, axis=1, keepdims=True)
            vals = block[:, 2 * inner + window : min(2 * inner + window + 256, 1792)]
            product = jnp.dot(expons.astype(BF), vals, preferred_element_type=F32) / totals
            near = lanes256[:, : vals.shape[1]] + window
            held = (near >= start) & (near < start + HEAD)
            spot = (slice(p * 96, p * 96 + 96), slice(window, window + vals.shape[1]))
            tm[spot] = jnp.where(held, product, tm[spot])

    back = jnp.dot(to_group, tm[...].astype(BF), preferred_element_type=F32)
    pf[:, 0:640] = back

    def cut_back(g):
        both = pf[eight(g), 0:640]
        sb2[2 * g] = both[0:4].astype(BF)
        sb2[2 * g + 1] = both[4:8].astype(BF)

    each(0, n // 2, cut_back)

    def home(i):
        target = lax.rem(f + i, n)
        return send(sb2.at[target], rb2.at[f], gs.at[i], gr.at[i], (target, s))

    each(1, n, lambda i: home(i).start())
    rb2[f] = sb2[f]
    each(1, n, lambda i: home(i).wait_recv())

    def gather_back(g):
        pf[eight(g), 0:640] = jnp.concatenate(
            [rb2[2 * g].astype(F32), rb2[2 * g + 1].astype(F32)], axis=0
        )

    each(0, n // 2, gather_back)
    final = jnp.dot(to_rows, pf[:, 0:640].astype(BF), preferred_element_type=F32)
    mix_out[...] = final[:, 0:inner].astype(BF).reshape(mix_out.shape)
    each(1, n, lambda i: forth(i).wait_send())
    each(1, n, lambda i: home(i).wait_send())


def per_device(residual_in, q_spatial, k_spatial, v_spatial, w_out, modulation, w_temporal):
    frames, places, features = residual_in.shape
    half = places // 2
    total = 16 * places
    vmem = pl.BlockSpec(memory_space=pltpu.VMEM)
    dma = pltpu.SemaphoreType.DMA
    mixed = pl.pallas_call(
        spatial_kernel,
        out_shape=jax.ShapeDtypeStruct((2, 8, places + 16, 128), BF),
        in_specs=[vmem] * 3,
        out_specs=vmem,
        scratch_shapes=[
            pltpu.VMEM((2, 8, places + half, 128), BF),
            pltpu.VMEM((2, 8, places, 128), BF),
            pltpu.VMEM((2, 8, places, 128), BF),
            pltpu.VMEM((8, places + half, 128), BF),
            pltpu.VMEM((8, places, 128), BF),
            pltpu.VMEM((8, places, 128), BF),
            pltpu.VMEM((16, places + half, 128), BF),
            pltpu.VMEM((16, places, 128), BF),
            pltpu.VMEM((16, places, 128), BF),
            pltpu.VMEM((total, 256), BF),
            pltpu.VMEM((total, 128), BF),
            pltpu.VMEM((total, 256), BF),
            pltpu.VMEM((total, 256), BF),
            pltpu.VMEM((2, total, total), BF),
            pltpu.VMEM((16, places + 16, 128), BF),
            pltpu.VMEM((8, places + 16, 128), BF),
            dma((3, 8)), dma((3, 8)), dma((2, 3, 8)), dma((2, 3, 8)),
            dma((8,)), dma((8,)), dma((2, 8)), dma((2, 8)),
        ],
        compiler_params=pltpu.CompilerParams(
            collective_id=1, has_side_effects=True, vmem_limit_bytes=40 << 20
        ),
        name="spatial_attention",
    )(q_spatial, k_spatial, v_spatial)
    width = w_temporal.shape[1]
    return pl.pallas_call(
        temporal_kernel,
        out_shape=(
            jax.ShapeDtypeStruct((frames, places, features), BF),
            jax.ShapeDtypeStruct((frames, places, width // 3), BF),
        ),
        in_specs=[vmem] * 5,
        out_specs=(vmem, vmem),
        scratch_shapes=[
            pltpu.VMEM((2 * places, features), BF),
            pltpu.VMEM((features, features), BF),
            pltpu.VMEM((2 * places, 1792), F32),
            pltpu.VMEM((48, 4, 1792), BF),
            pltpu.VMEM((48, 4, 1792), BF),
            pltpu.VMEM((2 * places, 640), F32),
            pltpu.VMEM((48, 4, 640), BF),
            pltpu.VMEM((48, 4, 640), BF),
            dma((48,)), dma((48,)), dma((48,)), dma((48,)),
        ],
        compiler_params=pltpu.CompilerParams(
            collective_id=2, has_side_effects=True, vmem_limit_bytes=40 << 20
        ),
        name="temporal_attention",
    )(mixed, residual_in, w_out, modulation, w_temporal)


def solution(mesh):
    return jax.shard_map(
        per_device,
        mesh=mesh,
        in_specs=(
            P("frame", "space", None),
            P("frame", "space", None),
            P("frame", "space", None),
            P("frame", "space", None),
            P(),
            P(),
            P(),
        ),
        out_specs=(P("frame", "space", None), P("frame", "space", None)),
        check_vma=False,
    )
```

time: 272 us -> 159 us (0.58)
  Pallas kernels: 0 us -> 144 us
  blocking collectives: 79.1 us -> 0 us
  waiting for transfers between devices: 62.8 us -> 0 us
  starting transfers between devices: 52.7 us -> 0 us
  local copies, waits for them, and re-layouts: 47.4 us -> 14 us
  matrix products: 23.7 us -> 0 us
  other arithmetic: 4.26 us -> 0 us
    pallas_call x0 -> x2, Pallas kernels: none -> 144 us  [the longest x1 76.7 us: per_device(): pl.pallas_call(spatial_kernel, out_shape=jax.ShapeDtypeStruct((2, 8, plac...]
    all_to_all x2 -> x0, blocking collectives: 79.1 us -> none  [the longest x1 58 us: per_device(): lax.all_to_all(projected, 'frame', split_axis=1, concat_axis=0, tiled=True)]
    all_to_all x4 -> x0, waiting for transfers between devices: 62.8 us -> none  [the longest x1 19.5 us: per_device(): lax.all_to_all(head_mix, 'space', split_axis=1, concat_axis=2, tiled=True)]
    all_to_all x4 -> x0, starting transfers between devices: 52.7 us -> none  [the longest x1 20.4 us: per_device(): lax.all_to_all(q_spatial, 'space', split_axis=2, concat_axis=1, tiled=True)]
    dot_general x16 -> x0, matrix products: 23.7 us -> none  [the longest x6 9.38 us: attend_block(): jnp.einsum('qha,kha->hqk', query_heads, key_heads, preferred_element_type...]
    while x6 -> x0, local copies, waits for them, and re-layouts: 14.4 us -> none  [the longest x4 12.1 us: spatial_heads_attend(): lax.map(lambda framed: frame_attend(framed[0], framed[1], framed[2], head...]
    reshape x3 -> x0, local copies, waits for them, and re-layouts: 7.3 us -> none  [the longest x2 4.25 us: per_device(): projected.astype(jnp.bfloat16)]
    all_to_all x5 -> x0, local copies, waits for them, and re-layouts: 5.22 us -> none  [the longest x1 1.84 us: per_device(): lax.all_to_all(head_mix, 'space', split_axis=1, concat_axis=2, tiled=True)]
  transfers between devices with their start and end apart: 4 -> 0, of which waited for: 4 -> 0; matrix products, arithmetic and copies ran while one was open for 4% -> 0% of each run, Pallas kernels for 0% -> 0%
where the time goes in v1:
time: 159 us
  Pallas kernels  144 us (91%)
  local copies, waits for them, and re-layouts  14 us (9%)
    pallas_call x1, Pallas kernels, per_device(): pl.pallas_call(spatial_kernel, out_shape=jax.ShapeDtypeStruct((2, 8, plac...  76.7 us
    pallas_call x1, Pallas kernels, per_device(): pl.pallas_call(temporal_kernel, out_shape=(jax.ShapeDtypeStruct((frames,...  67.4 us
    unnamed x17, local copies, waits for them, and re-layouts  14 us

profile of v1, /device:TPU:1, one launch (start us, length us, event | category | flops | bytes accessed | tf_op | source)
XLA Modules:
  0.0 158.8 jit_solution(9193403145798356949)
XLA Ops:
  0.6 0.0 copy-start.2
  0.6 1.0 copy-done.2
  1.6 0.0 copy-start.3
  1.6 1.0 copy-done.3
  2.7 0.0 copy-start.4
  2.7 1.0 copy-done.4
  3.7 76.7 %spatial_attention.1.mix_ref = bf16[2,8,112,128]{3,2,1,0:T(8,128)(2,1)S(1)} custom-call(bf16[2,96,1152]{2,1,0:T(8,128)(2,1)S(1)} %copy-done.2, bf16[2,96,1152]{2,1,0:T(8,128)(2,1)S(1)} %copy-done.3, bf16[2,96,1152]{2,1,0:T(8,128)(2,1)S(1)} %copy-done.4), custom_call_target="tpu_custom_call" | custom-call | tf_op jit(solution)/shard_map/spatial_attention/pallas_call | solution.py:457
  80.4 0.0 copy-start.1
  80.4 0.0 copy-start.5
  80.4 6.6 %copy.9.wt_ref = bf16[1152,1728]{1,0:T(8,128)(2,1)} copy(bf16[1152,1728]{0,1:T(8,128)(2,1)} %param.13) | data formatting | bytes 7962624 | tf_op args[6]
  87.0 0.0 copy-done.1
  87.0 0.0 copy-done.5
  87.0 0.0 copy-start
  87.0 2.2 %copy-done = bf16[1152,1728]{1,0:T(8,128)(2,1)S(1)} copy-done((bf16[1152,1728]{1,0:T(8,128)(2,1)S(1)}, bf16[1152,1728]{1,0:T(8,128)(2,1)}, u32[]{:S(2)}) %copy-start) | copy-done | bytes 3981336
  89.2 0.0 copy-start.6
  89.2 0.7 copy-done.6
  89.9 67.4 %temporal_attention.1 = (bf16[2,96,1152]{2,1,0:T(8,128)(2,1)S(1)}, bf16[2,96,576]{2,1,0:T(8,128)(2,1)S(1)}) custom-call(bf16[2,8,112,128]{3,2,1,0:T(8,128)(2,1)S(1)} %spatial_attention.1.mix_ref, bf16[2,96,1152]{2,1,0:T(8,128)(2,1)S(1)} %copy-done.5, bf16[1152,1152]{1,0:T(8,128)(2,1)S(1)} %copy-done.1, f32[3,1152]{1,0:T(4,128)S(1)} %copy-done.6, ...), custom_call_target="tpu_custom_call" | custom-call | tf_op jit(solution)/shard_map/temporal_attention/pallas_call | solution.py:488
  157.3 0.8 copy.12
  158.1 0.7 copy.13
Async XLA Ops:
  0.6 1.0 copy-start.2
  1.6 1.0 copy-start.3
  2.7 1.0 copy-start.4
  80.4 6.6 %copy-start.1 = (bf16[1152,1152]{1,0:T(8,128)(2,1)S(1)}, bf16[1152,1152]{1,0:T(8,128)(2,1)}, u32[]{:S(2)}) copy-start(bf16[1152,1152]{1,0:T(8,128)(2,1)} %wo_ref.1) | copy-start | bytes 7962628
  80.4 6.6 %copy-start.5 = (bf16[2,96,1152]{2,1,0:T(8,128)(2,1)S(1)}, bf16[2,96,1152]{2,1,0:T(8,128)(2,1)}, u32[]{:S(2)}) copy-start(bf16[2,96,1152]{2,1,0:T(8,128)(2,1)} %res_ref.1) | copy-start | bytes 1327108
  87.0 2.2 %copy-start = (bf16[1152,1728]{1,0:T(8,128)(2,1)S(1)}, bf16[1152,1728]{1,0:T(8,128)(2,1)}, u32[]{:S(2)}) copy-start(bf16[1152,1728]{1,0:T(8,128)(2,1)} %copy.9.wt_ref) | copy-start | bytes 11943940
  89.2 0.7 copy-start.6

commit v2 on v1

--- a/solution.py
+++ b/solution.py
@@ -13,6 +13,7 @@
 T_HEADS = 8
 BF = jnp.bfloat16
 F32 = jnp.float32
+ORDER = (3, 2, 4, 1, 5)
 EXP2_SCALE = math.log2(math.e) / math.sqrt(HEAD)
 
 
@@ -33,10 +34,19 @@
     )
 
 
-def spatial_kernel(
-    q_ref, k_ref, v_ref, out_ref,
-    sbk, sbq, sbv, zrk, zrq, zrv, fk, fq, fv, qs, k0, k1, vs, pr, ob, zro,
-    zs, zr, ys, yr, zos, zor, yos, yor,
+def one_hot(rows_of):
+    size = 192
+    row = lax.broadcasted_iota(jnp.int32, (size, size), 0)
+    column = lax.broadcasted_iota(jnp.int32, (size, size), 1)
+    return jnp.where(column == rows_of(row), 1.0, 0.0).astype(BF)
+
+
+def block_kernel(
+    res_hbm, q_hbm, k_hbm, v_hbm, wo_hbm, mod_ref, wt_hbm, res_out, mix_out,
+    q_ref, k_ref, v_ref, res_ref, wp, wt,
+    sbk, sbq, sbv, zrk, zrq, zrv, fk, fq, fv, qs, k0, k1, vs, pr, ob, zro, mixb,
+    am, pf, sb, zx, rb, tm, sb2, zx2, rb2,
+    ld, zs, zr, ys, yr, zos, zor, yos, yor, ts, tr, xs, xr, us, ur, ws, wr,
 ):
     f = lax.axis_index("frame")
     s = lax.axis_index("space")
@@ -45,6 +55,35 @@
     far = 1 - a
     partner = (f, far * 8 + y)
     places = q_ref.shape[1]
+    core = lax.rem(f, 2)
+    z = lax.rem(f // 2, 6)
+    kme = (f // 12) * 2 + core
+
+    def peer(k, level):
+        return (((k // 2) * 6 + level) * 2 + lax.rem(k, 2), s)
+
+    loads = [
+        pltpu.make_async_copy(k_hbm, k_ref, ld.at[0]),
+        pltpu.make_async_copy(q_hbm, q_ref, ld.at[1]),
+        pltpu.make_async_copy(v_hbm, v_ref, ld.at[2]),
+        pltpu.make_async_copy(res_hbm, res_ref, ld.at[3]),
+        pltpu.make_async_copy(wt_hbm, wt, ld.at[4]),
+    ]
+    for pair in range(8):
+        loads.append(
+            pltpu.make_async_copy(
+                wo_hbm.at[pl.ds(144 * pair, 128)], wp.at[pl.ds(128 * pair, 128)], ld.at[5 + 2 * pair]
+            )
+        )
+        loads.append(
+            pltpu.make_async_copy(
+                wo_hbm.at[pl.ds(144 * pair + 128, 16)],
+                wp.at[pl.ds(1024 + 16 * pair, 16)],
+                ld.at[6 + 2 * pair],
+            )
+        )
+    for load in loads[:3]:
+        load.start()
     half = places // 2
 
     barrier = pltpu.get_barrier_semaphore()
@@ -57,6 +96,26 @@
         return carry
 
     lax.fori_loop(1, 8, greet, 0)
+
+    def greet_level(j, carry):
+        pl.semaphore_signal(
+            barrier, inc=1, device_id=peer(kme, lax.rem(z + j, 6)), device_id_type=MESH
+        )
+        return carry
+
+    lax.fori_loop(1, 6, greet_level, 0)
+
+    def greet_row(j, carry):
+        pl.semaphore_signal(
+            barrier, inc=1, device_id=peer(lax.rem(kme + j, 8), z), device_id_type=MESH
+        )
+        return carry
+
+    lax.fori_loop(1, 8, greet_row, 0)
+    for load in loads[:3]:
+        load.wait()
+    for load in loads[3:]:
+        load.start()
 
     lanes = lane_iota(places)
     half_lanes = lane_iota(half)
@@ -124,7 +183,7 @@
         lax.fori_loop(low, high, step, 0)
 
     pack_k(far)
-    pl.semaphore_wait(barrier, 8)
+    pl.semaphore_wait(barrier, 20)
 
     def z_start(t):
         each(1, 8, lambda j: z_copy(t, j).start())
@@ -236,19 +295,19 @@
         )
 
     def z_back_home():
-        return send(ob.at[far * 8 + y], out_ref.at[a, y], zos.at[y], zor.at[y], partner)
+        return send(ob.at[far * 8 + y], mixb.at[1, y], zos.at[y], zor.at[y], partner)
 
     def y_back(j):
         target = lax.rem(y + j, 8)
         return send(
-            ob.at[a * 8 + target], out_ref.at[a, y], yos.at[0, j], yor.at[0, j],
+            ob.at[a * 8 + target], mixb.at[0, y], yos.at[0, j], yor.at[0, j],
             (f, a * 8 + target),
         )
 
     def y_back_relay(target):
         j = lax.rem(target + 8 - y, 8)
         return send(
-            zro.at[target], out_ref.at[far, y], yos.at[1, j], yor.at[1, j], (f, a * 8 + target)
+            zro.at[target], mixb.at[1, y], yos.at[1, j], yor.at[1, j], (f, a * 8 + target)
         )
 
     def z_back_start(target):
@@ -270,8 +329,86 @@
     each(0, 2, far_part)
     each(0, 2, near_part)
     each(1, 8, lambda j: y_back(j).start())
-    out_ref[a, y] = ob[s]
-
+    mixb[0, y] = ob[s]
+
+    for load in loads[3:]:
+        load.wait()
+
+    def project(kind, frame):
+        packs = [mixb[kind, pair, places : places + 16].astype(F32) for pair in range(8)]
+        for pair in range(8):
+            am[kind, :, 128 * pair : 128 * pair + 128] = mixb[kind, pair, 0:places]
+        for group in range(6):
+            joined = roll_lanes(packs[0], -16 * group)
+            for pair in range(1, 8):
+                moved = roll_lanes(packs[pair], 16 * pair - 16 * group)
+                joined = jnp.where(sub_lanes < 16 * pair, joined, moved)
+            am[kind, 16 * group : 16 * group + 16, 1024:1152] = joined.astype(BF)
+        branch = jnp.dot(am[kind], wp[...], preferred_element_type=F32)
+        res = (res_ref[frame].astype(F32) + mod_ref[2:3, :] * branch).astype(BF)
+        res_out[frame] = res
+        values = res.astype(F32)
+        center = jnp.mean(values, axis=1, keepdims=True)
+        moved = values - center
+        deviation = jnp.mean(moved * moved, axis=1, keepdims=True)
+        normed = moved * lax.rsqrt(deviation + 1e-06) * (1.0 + mod_ref[1:2, :]) + mod_ref[0:1, :]
+        pf[0:places, 0:width] = lax.dot_general(
+            normed.astype(BF), wt[...], (((1,), (1,)), ((), ())), preferred_element_type=F32
+        )
+
+        def cut(g):
+            eight = pf[pl.ds(pl.multiple_of(8 * g, 8), 8), :]
+            for t in range(4):
+                sb[kind, 4 * g + t] = eight[2 * t : 2 * t + 2].astype(BF)
+
+        each(0, places // 8, cut)
+
+    def level_copy(kind, j):
+        level = lax.rem(z + j, 6)
+        return send(
+            sb.at[kind, pl.ds(8 * level, 8)], zx.at[kind, z], ts.at[kind, level], tr.at[kind, z],
+            peer(kme, level),
+        )
+
+    def level_arrival(kind, level):
+        return send(
+            sb.at[kind, pl.ds(0, 8)], zx.at[kind, level], ts.at[kind, level], tr.at[kind, level],
+            peer(kme, level),
+        )
+
+    def row_copy(kind, level, j, own):
+        k = lax.rem(kme + j, 8)
+        source = sb.at[kind, 8 * z + k] if own else zx.at[kind, level, k]
+        return send(
+            source, rb.at[kind, level * 8 + kme], xs.at[kind, level, k], xr.at[kind, level, kme],
+            peer(k, z),
+        )
+
+    def row_arrival(kind, level, j):
+        k = lax.rem(kme + j, 8)
+        return send(
+            sb.at[kind, 0], rb.at[kind, level * 8 + k], xs.at[kind, level, k],
+            xr.at[kind, level, k], peer(k, z),
+        )
+
+    def exchange(kind):
+        for j in ORDER:
+            level_copy(kind, j).start()
+        each(1, 8, lambda j: row_copy(kind, z, j, True).start())
+        rb[kind, 8 * z + kme] = sb[kind, 8 * z + kme]
+
+    def relay_level(kind, j):
+        level = lax.rem(z + j, 6)
+        level_arrival(kind, level).wait_recv()
+        each(1, 8, lambda i: row_copy(kind, level, i, False).start())
+        rb[kind, 8 * level + kme] = zx[kind, level, kme]
+
+    each(1, 8, lambda j: y_back(j).wait_recv())
+    width = wt.shape[0]
+    inner = width // 3
+    pf[:, 1664:1792] = jnp.zeros((2 * places, 128), F32)
+    project(0, a)
+    exchange(0)
     def relay_back(target):
         @pl.when(target != y)
         def _():
@@ -280,11 +417,10 @@
 
     each(0, 8, relay_back)
     z_back_home().wait_recv()
-    each(1, 8, lambda j: y_back(j).wait_recv())
 
     def relay_end(j):
         copy = send(
-            zro.at[0], out_ref.at[far, 0], yos.at[1, j], yor.at[1, j], (f, a * 8 + lax.rem(y + j, 8))
+            zro.at[0], mixb.at[1, 0], yos.at[1, j], yor.at[1, j], (f, a * 8 + lax.rem(y + j, 8))
         )
         copy.wait_recv()
         copy.wait_send()
@@ -292,108 +428,32 @@
     each(1, 8, relay_end)
     each(1, 8, lambda j: y_back(j).wait_send())
 
-    each(0, 8, lambda target: z_back(target).wait_send())
-    for t in range(3):
-        z_home(t).wait_send()
-        each(1, 8, lambda j: z_copy(t, j).wait_send())
-        each(1, 8, lambda j: y_copy(t, j).wait_send())
-        each(1, 8, lambda j: y_relay(t, j).wait_send())
-
-
-def one_hot(rows_of):
-    size = 192
-    row = lax.broadcasted_iota(jnp.int32, (size, size), 0)
-    column = lax.broadcasted_iota(jnp.int32, (size, size), 1)
-    return jnp.where(column == rows_of(row), 1.0, 0.0).astype(BF)
-
-
-def temporal_kernel(
-    mix_ref, res_ref, wo_ref, mod_ref, wt_ref, res_out, mix_out,
-    am, wp, pf, sbf, rbf, tm, sb2, rb2, fs, fr_sem, gs, gr,
-):
-    f = lax.axis_index("frame")
-    s = lax.axis_index("space")
-    n = lax.axis_size("frame")
-    barrier = pltpu.get_barrier_semaphore()
-
-    def each(low, high, body):
-        def step(j, carry):
-            body(j)
-            return carry
-
-        lax.fori_loop(low, high, step, 0)
-
-    each(
-        1, n,
-        lambda i: pl.semaphore_signal(
-            barrier, inc=1, device_id=(lax.rem(f + i, n), s), device_id_type=MESH
-        ),
+    project(1, far)
+    exchange(1)
+    for kind in range(2):
+        for j in ORDER:
+            relay_level(kind, 6 - j)
+
+    def gather(kind, level):
+        each(1, 8, lambda j: row_arrival(kind, level, j).wait_recv())
+        for half_row in range(2):
+            parts = [rb[kind, 8 * level + 4 * half_row + t].astype(F32) for t in range(4)]
+            start = pl.multiple_of(kind * 96 + 16 * level + 8 * half_row, 8)
+            pf[pl.ds(start, 8), :] = jnp.concatenate(parts, axis=0)
+
+    for kind in range(2):
+        for j in (0,) + ORDER:
+            gather(kind, lax.rem(z + 6 - j, 6))
+
+    by_place = one_hot(
+        lambda r: (lax.rem(r, 96) // 48) * 96 + 2 * lax.rem(r, 48) + r // 96
     )
-
-    places = res_ref.shape[1]
-    width = wt_ref.shape[1]
-    inner = width // 3
-    lanes16 = lane_iota(16)
-    for pair in range(8):
-        wp[128 * pair : 128 * pair + 128] = wo_ref[144 * pair : 144 * pair + 128]
-        wp[1024 + 16 * pair : 1040 + 16 * pair] = wo_ref[144 * pair + 128 : 144 * pair + 144]
-    for frame in range(2):
-        base = frame * places
-        for pair in range(8):
-            am[base : base + places, 128 * pair : 128 * pair + 128] = mix_ref[frame, pair, 0:places]
-        packs = [mix_ref[frame, pair, places : places + 16].astype(F32) for pair in range(8)]
-        for group in range(6):
-            joined = roll_lanes(packs[0], -16 * group)
-            for pair in range(1, 8):
-                moved = roll_lanes(packs[pair], 16 * pair - 16 * group)
-                joined = jnp.where(lanes16 < 16 * pair, joined, moved)
-            am[base + 16 * group : base + 16 * group + 16, 1024:1152] = joined.astype(BF)
-
-    branch = jnp.dot(am[...], wp[...], preferred_element_type=F32)
-    res = res_ref[...].reshape(2 * places, res_ref.shape[2]).astype(F32)
-    res = (res + mod_ref[2:3, :] * branch).astype(BF)
-    res_out[...] = res.reshape(res_out.shape)
-    values = res.astype(F32)
-    center = jnp.mean(values, axis=1, keepdims=True)
-    moved = values - center
-    spread = jnp.mean(moved * moved, axis=1, keepdims=True)
-    normed = moved * lax.rsqrt(spread + 1e-06) * (1.0 + mod_ref[1:2, :]) + mod_ref[0:1, :]
-    normed = normed.astype(BF)
-
-    by_group = one_hot(lambda r: lax.rem(r, 2) * 96 + 2 * (r // 4) + lax.rem(r // 2, 2))
-    by_place = one_hot(lambda r: 4 * (lax.rem(r, 96) // 2) + 2 * (r // 96) + lax.rem(r, 2))
-    to_group = one_hot(lambda r: lax.rem(r // 2, 2) * 96 + 2 * (r // 4) + lax.rem(r, 2))
-    to_rows = one_hot(lambda r: 4 * (lax.rem(r, 96) // 2) + 2 * lax.rem(r, 2) + r // 96)
-
-    grouped = jnp.dot(by_group, normed, preferred_element_type=F32).astype(BF)
-    pf[:, 1664:1792] = jnp.zeros((2 * places, 128), F32)
-    pf[:, 0:width] = jnp.dot(grouped, wt_ref[...], preferred_element_type=F32)
-
-    def eight(g):
-        return pl.ds(pl.multiple_of(8 * g, 8), 8)
-
-    def cut(g):
-        both = pf[eight(g), :]
-        sbf[2 * g] = both[0:4].astype(BF)
-        sbf[2 * g + 1] = both[4:8].astype(BF)
-
-    each(0, n // 2, cut)
-    pl.semaphore_wait(barrier, n - 1)
-
-    def forth(i):
-        target = lax.rem(f + i, n)
-        return send(sbf.at[target], rbf.at[f], fs.at[i], fr_sem.at[i], (target, s))
-
-    each(1, n, lambda i: forth(i).start())
-    rbf[f] = sbf[f]
-    each(1, n, lambda i: forth(i).wait_recv())
-
-    def gather(g):
-        pf[eight(g), :] = jnp.concatenate(
-            [rbf[2 * g].astype(F32), rbf[2 * g + 1].astype(F32)], axis=0
-        )
-
-    each(0, n // 2, gather)
+    to_group = one_hot(
+        lambda r: lax.rem(r, 2) * 96 + lax.rem(r // 2, 2) * 48 + r // 4
+    )
+    to_rows = one_hot(
+        lambda r: 4 * (lax.rem(r, 96) // 2) + 2 * (r // 96) + lax.rem(r, 2)
+    )
     rows = jnp.dot(by_place, pf[...].astype(BF), preferred_element_type=F32).astype(BF)
     lanes256 = lax.broadcasted_iota(jnp.int32, (96, 256), 1)
     tm[...] = jnp.zeros(tm.shape, F32)
@@ -403,8 +463,7 @@
             start = head * HEAD
             queries = block[:, start : start + HEAD]
             keys = block[:, inner + start : inner + start + HEAD]
-            window = (start // 128) * 128
-            window = min(window, 384)
+            window = min((start // 128) * 128, 384)
             scores = lax.dot_general(
                 queries, keys, (((1,), (1,)), ((), ())), preferred_element_type=F32
             )
@@ -418,48 +477,110 @@
             spot = (slice(p * 96, p * 96 + 96), slice(window, window + vals.shape[1]))
             tm[spot] = jnp.where(held, product, tm[spot])
 
-    back = jnp.dot(to_group, tm[...].astype(BF), preferred_element_type=F32)
-    pf[:, 0:640] = back
+    pf[:, 0:640] = jnp.dot(to_group, tm[...].astype(BF), preferred_element_type=F32)
 
     def cut_back(g):
-        both = pf[eight(g), 0:640]
+        both = pf[pl.ds(pl.multiple_of(8 * g, 8), 8), 0:640]
         sb2[2 * g] = both[0:4].astype(BF)
         sb2[2 * g + 1] = both[4:8].astype(BF)
 
-    each(0, n // 2, cut_back)
-
-    def home(i):
-        target = lax.rem(f + i, n)
-        return send(sb2.at[target], rb2.at[f], gs.at[i], gr.at[i], (target, s))
-
-    each(1, n, lambda i: home(i).start())
-    rb2[f] = sb2[f]
-    each(1, n, lambda i: home(i).wait_recv())
-
-    def gather_back(g):
-        pf[eight(g), 0:640] = jnp.concatenate(
-            [rb2[2 * g].astype(F32), rb2[2 * g + 1].astype(F32)], axis=0
-        )
-
-    each(0, n // 2, gather_back)
+    each(0, 24, cut_back)
+
+    def level_home(j):
+        level = lax.rem(z + j, 6)
+        return send(
+            sb2.at[pl.ds(8 * level, 8)], zx2.at[z], us.at[level], ur.at[z], peer(kme, level)
+        )
+
+    def level_home_arrival(level):
+        return send(
+            sb2.at[pl.ds(0, 8)], zx2.at[level], us.at[level], ur.at[level], peer(kme, level)
+        )
+
+    def row_home(level, j, own):
+        k = lax.rem(kme + j, 8)
+        source = sb2.at[8 * z + k] if own else zx2.at[level, k]
+        return send(
+            source, rb2.at[level * 8 + kme], ws.at[level, k], wr.at[level, kme], peer(k, z)
+        )
+
+    def row_home_arrival(level, j):
+        k = lax.rem(kme + j, 8)
+        return send(
+            sb2.at[0], rb2.at[level * 8 + k], ws.at[level, k], wr.at[level, k], peer(k, z)
+        )
+
+    for j in ORDER:
+        level_home(j).start()
+    each(1, 8, lambda j: row_home(z, j, True).start())
+    rb2[8 * z + kme] = sb2[8 * z + kme]
+    for j in ORDER:
+        level = lax.rem(z + 6 - j, 6)
+        level_home_arrival(level).wait_recv()
+        each(1, 8, lambda i: row_home(level, i, False).start())
+        rb2[8 * level + kme] = zx2[level, kme]
+
+    def gather_back(level):
+        each(1, 8, lambda j: row_home_arrival(level, j).wait_recv())
+        for part in range(4):
+            start = pl.multiple_of(32 * level + 8 * part, 8)
+            pair = 8 * level + 2 * part
+            pf[pl.ds(start, 8), 0:640] = jnp.concatenate(
+                [rb2[pair].astype(F32), rb2[pair + 1].astype(F32)], axis=0
+            )
+
+    for j in (0,) + ORDER:
+        gather_back(lax.rem(z + 6 - j, 6))
     final = jnp.dot(to_rows, pf[:, 0:640].astype(BF), preferred_element_type=F32)
-    mix_out[...] = final[:, 0:inner].astype(BF).reshape(mix_out.shape)
-    each(1, n, lambda i: forth(i).wait_send())
-    each(1, n, lambda i: home(i).wait_send())
+    mix_out[a] = final[0:96, 0:inner].astype(BF)
+    mix_out[far] = final[96:192, 0:inner].astype(BF)
+
+    for j in ORDER:
+        for kind in range(2):
+            level_copy(kind, j).wait_send()
+        level_home(j).wait_send()
+
+    def drain(level):
+        def one(j):
+            for kind in range(2):
+                row_copy(kind, level, j, False).wait_send()
+            row_home(level, j, False).wait_send()
+
+        each(1, 8, one)
+
+    each(0, 6, drain)
+    each(0, 8, lambda target: z_back(target).wait_send())
+    for t in range(3):
+        z_home(t).wait_send()
+        each(1, 8, lambda j: z_copy(t, j).wait_send())
+        each(1, 8, lambda j: y_copy(t, j).wait_send())
+        each(1, 8, lambda j: y_relay(t, j).wait_send())
 
 
 def per_device(residual_in, q_spatial, k_spatial, v_spatial, w_out, modulation, w_temporal):
     frames, places, features = residual_in.shape
     half = places // 2
     total = 16 * places
+    width = w_temporal.shape[1]
     vmem = pl.BlockSpec(memory_space=pltpu.VMEM)
+    hbm = pl.BlockSpec(memory_space=pl.ANY)
     dma = pltpu.SemaphoreType.DMA
-    mixed = pl.pallas_call(
-        spatial_kernel,
-        out_shape=jax.ShapeDtypeStruct((2, 8, places + 16, 128), BF),
-        in_specs=[vmem] * 3,
-        out_specs=vmem,
+    local = (frames, places, features)
+    return pl.pallas_call(
+        block_kernel,
+        out_shape=(
+            jax.ShapeDtypeStruct(local, BF),
+            jax.ShapeDtypeStruct((frames, places, width // 3), BF),
+        ),
+        in_specs=[hbm] * 5 + [vmem, hbm],
+        out_specs=(vmem, vmem),
         scratch_shapes=[
+            pltpu.VMEM(local, BF),
+            pltpu.VMEM(local, BF),
+            pltpu.VMEM(local, BF),
+            pltpu.VMEM(local, BF),
+            pltpu.VMEM((features, features), BF),
+            pltpu.VMEM((width, features), BF),
             pltpu.VMEM((2, 8, places + half, 128), BF),
             pltpu.VMEM((2, 8, places, 128), BF),
             pltpu.VMEM((2, 8, places, 128), BF),
@@ -476,39 +597,27 @@
             pltpu.VMEM((2, total, total), BF),
             pltpu.VMEM((16, places + 16, 128), BF),
             pltpu.VMEM((8, places + 16, 128), BF),
+            pltpu.VMEM((2, 8, places + 16, 128), BF),
+            pltpu.VMEM((2, places, features), BF),
+            pltpu.VMEM((2 * places, 1792), F32),
+            pltpu.VMEM((2, 48, 2, 1792), BF),
+            pltpu.VMEM((2, 6, 8, 2, 1792), BF),
+            pltpu.VMEM((2, 48, 2, 1792), BF),
+            pltpu.VMEM((2 * places, 640), F32),
+            pltpu.VMEM((48, 4, 640), BF),
+            pltpu.VMEM((6, 8, 4, 640), BF),
+            pltpu.VMEM((48, 4, 640), BF),
+            dma((21,)),
             dma((3, 8)), dma((3, 8)), dma((2, 3, 8)), dma((2, 3, 8)),
             dma((8,)), dma((8,)), dma((2, 8)), dma((2, 8)),
+            dma((2, 6)), dma((2, 6)), dma((2, 6, 8)), dma((2, 6, 8)),
+            dma((6,)), dma((6,)), dma((6, 8)), dma((6, 8)),
         ],
         compiler_params=pltpu.CompilerParams(
-            collective_id=1, has_side_effects=True, vmem_limit_bytes=40 << 20
+            collective_id=1, has_side_effects=True, vmem_limit_bytes=52 << 20
         ),
-        name="spatial_attention",
-    )(q_spatial, k_spatial, v_spatial)
-    width = w_temporal.shape[1]
-    return pl.pallas_call(
-        temporal_kernel,
-        out_shape=(
-            jax.ShapeDtypeStruct((frames, places, features), BF),
-            jax.ShapeDtypeStruct((frames, places, width // 3), BF),
-        ),
-        in_specs=[vmem] * 5,
-        out_specs=(vmem, vmem),
-        scratch_shapes=[
-            pltpu.VMEM((2 * places, features), BF),
-            pltpu.VMEM((features, features), BF),
-            pltpu.VMEM((2 * places, 1792), F32),
-            pltpu.VMEM((48, 4, 1792), BF),
-            pltpu.VMEM((48, 4, 1792), BF),
-            pltpu.VMEM((2 * places, 640), F32),
-            pltpu.VMEM((48, 4, 640), BF),
-            pltpu.VMEM((48, 4, 640), BF),
-            dma((48,)), dma((48,)), dma((48,)), dma((48,)),
-        ],
-        compiler_params=pltpu.CompilerParams(
-            collective_id=2, has_side_effects=True, vmem_limit_bytes=40 << 20
-        ),
-        name="temporal_attention",
-    )(mixed, residual_in, w_out, modulation, w_temporal)
+        name="block",
+    )(residual_in, q_spatial, k_spatial, v_spatial, w_out, modulation, w_temporal.T)
 
 
 def solution(mesh):

time: 159 us -> 146 us (0.918)
  the two profiles are of different devices: /device:TPU:1 before, /device:TPU:57 now
where the time goes in v2:
time: 146 us
  Pallas kernels  141 us (97%)
  local copies, waits for them, and re-layouts  4.2 us (3%)
    pallas_call x1, Pallas kernels, per_device(): pl.pallas_call(block_kernel, out_shape=(jax.ShapeDtypeStruct(local, BF),...  141 us
    unnamed x8, local copies, waits for them, and re-layouts  4.2 us

profile of v2, /device:TPU:57, one launch (start us, length us, event | category | flops | bytes accessed | tf_op | source)
XLA Modules:
  0.0 145.9 jit_solution(3077155722652131968)
XLA Ops:
  0.6 0.0 copy-start
  0.6 1.0 copy-done
  1.6 0.0 copy-start.1
  1.6 1.0 copy-done.1
  2.7 0.0 copy-start.2
  2.7 0.7 copy-done.2
  3.4 141.0 %block.1 = (bf16[2,96,1152]{2,1,0:T(8,128)(2,1)S(1)}, bf16[2,96,576]{2,1,0:T(8,128)(2,1)S(1)}) custom-call(bf16[2,96,1152]{2,1,0:T(8,128)(2,1)S(1)} %copy-done, bf16[2,96,1152]{2,1,0:T(8,128)(2,1)S(1)} %copy-done.1, bf16[2,96,1152]{2,1,0:T(8,128)(2,1)} %k_hbm.1, bf16[2,96,1152]{2,1,0:T(8,128)(2,1)} %v_hbm.1, bf16[1152,1152]{1,0:T(8,128)(2,1)} %wo_hbm.1, ...), custom_call_target="tpu_custom_call" | custom-call | tf_op jit(solution)/shard_map/block/pallas_call | solution.py:569
  144.4 0.8 copy.11
  145.2 0.7 copy.12
Async XLA Ops:
  0.6 1.0 copy-start
  1.6 1.0 copy-start.1
  2.7 0.7 copy-start.2

commit v3 on v2

--- a/solution.py
+++ b/solution.py
@@ -44,7 +44,7 @@
 def block_kernel(
     res_hbm, q_hbm, k_hbm, v_hbm, wo_hbm, mod_ref, wt_hbm, res_out, mix_out,
     q_ref, k_ref, v_ref, res_ref, wp, wt,
-    sbk, sbq, sbv, zrk, zrq, zrv, fk, fq, fv, qs, k0, k1, vs, pr, ob, zro, mixb,
+    sba, sbb, zra, zrb, fa, fb, qs, ks, vs, ob, zro, mixb,
     am, pf, sb, zx, rb, tm, sb2, zx2, rb2,
     ld, zs, zr, ys, yr, zos, zor, yos, yor, ts, tr, xs, xr, us, ur, ws, wr,
 ):
@@ -69,17 +69,12 @@
         pltpu.make_async_copy(res_hbm, res_ref, ld.at[3]),
         pltpu.make_async_copy(wt_hbm, wt, ld.at[4]),
     ]
-    for pair in range(8):
+    for head in range(16):
         loads.append(
             pltpu.make_async_copy(
-                wo_hbm.at[pl.ds(144 * pair, 128)], wp.at[pl.ds(128 * pair, 128)], ld.at[5 + 2 * pair]
-            )
-        )
-        loads.append(
-            pltpu.make_async_copy(
-                wo_hbm.at[pl.ds(144 * pair + 128, 16)],
-                wp.at[pl.ds(1024 + 16 * pair, 16)],
-                ld.at[6 + 2 * pair],
+                wo_hbm.at[pl.ds(HEAD * head, HEAD)],
+                wp.at[pl.ds(128 * head, HEAD)],
+                ld.at[5 + head],
             )
         )
     for load in loads[:3]:
@@ -116,6 +111,8 @@
         load.wait()
     for load in loads[3:]:
         load.start()
+    for head in range(16):
+        wp[128 * head + HEAD : 128 * head + 128] = jnp.zeros((128 - HEAD, wp.shape[1]), BF)
 
     lanes = lane_iota(places)
     half_lanes = lane_iota(half)
@@ -123,33 +120,45 @@
     def tile(ref, fr, index):
         return ref[fr, :, 128 * index : 128 * index + 128].astype(F32)
 
-    def main_of(ref, fr, pair):
-        low = tile(ref, fr, pair)
-        if pair == 0:
-            return low.astype(BF)
-        high = tile(ref, fr, pair + 1)
-        return roll_lanes(jnp.where(lanes >= 16 * pair, low, high), -16 * pair).astype(BF)
-
-    def pack_k(fr):
+    def piece(ref, fr, column, count, target):
+        index, offset = column // 128, column % 128
+        value = tile(ref, fr, index)
+        if offset + count > 128:
+            value = jnp.where(lanes >= offset, value, tile(ref, fr, index + 1))
+        return roll_lanes(value, target - offset)
+
+    def pack_first(fr):
         for pair in range(8):
-            sbk[fr, pair, 0:places] = main_of(k_ref, fr, pair)
-            left = jnp.where(
+            c = 144 * pair
+            one = jnp.where(
+                lanes < 72, piece(q_ref, fr, c, 72, 0), piece(k_ref, fr, c, 56, 72)
+            )
+            two = jnp.where(
                 lanes < 16,
-                roll_lanes(tile(k_ref, fr, pair + 1), -16 * pair),
+                piece(k_ref, fr, c + 56, 16, 0),
                 jnp.where(
-                    lanes < 32,
-                    roll_lanes(tile(q_ref, fr, pair + 1), 16 - 16 * pair),
-                    roll_lanes(tile(v_ref, fr, pair + 1), 32 - 16 * pair),
+                    lanes < 88, piece(v_ref, fr, c, 72, 16), piece(q_ref, fr, c + 72, 40, 88)
                 ),
             )
+            sba[fr, pair, 0:places] = one.astype(BF)
+            sba[fr, pair, places : 2 * places] = two.astype(BF)
+
+    def pack_second(fr):
+        for pair in range(8):
+            c = 144 * pair + 72
+            three = jnp.where(
+                lanes < 32,
+                piece(q_ref, fr, c + 40, 32, 0),
+                jnp.where(
+                    lanes < 104, piece(k_ref, fr, c, 72, 32), piece(v_ref, fr, c, 24, 104)
+                ),
+            )
+            left = piece(v_ref, fr, c + 24, 48, 0)
             joined = jnp.where(half_lanes < 64, left[0:half], roll_lanes(left[half:places], 64))
-            sbk[fr, pair, places : places + half] = joined.astype(BF)
-
-    def pack(ref, buf, fr):
-        for pair in range(8):
-            buf[fr, pair] = main_of(ref, fr, pair)
-
-    sent = ((sbk, zrk, fk), (sbq, zrq, fq), (sbv, zrv, fv))
+            sbb[fr, pair, 0:places] = three.astype(BF)
+            sbb[fr, pair, places : places + half] = joined.astype(BF)
+
+    sent = ((sba, zra, fa), (sbb, zrb, fb))
 
     def z_copy(t, j):
         buf, relay, final = sent[t]
@@ -182,7 +191,7 @@
 
         lax.fori_loop(low, high, step, 0)
 
-    pack_k(far)
+    pack_first(far)
     pl.semaphore_wait(barrier, 20)
 
     def z_start(t):
@@ -193,19 +202,14 @@
         each(1, 8, lambda j: y_copy(t, j).start())
 
     z_start(0)
-    pack(q_ref, sbq, far)
+    pack_second(far)
     z_start(1)
-    pack(v_ref, sbv, far)
-    z_start(2)
-    pack_k(a)
+    pack_first(a)
     y_start(0)
-    pack(q_ref, sbq, a)
+    pack_second(a)
     y_start(1)
-    pack(v_ref, sbv, a)
-    y_start(2)
-    fk[s] = sbk[a, y]
-    fq[s] = sbq[a, y]
-    fv[s] = sbv[a, y]
+    fa[s] = sba[a, y]
+    fb[s] = sbb[a, y]
 
     def forward(t, j):
         z_copy(t, j).wait_recv()
@@ -216,134 +220,149 @@
         each(1, 8, lambda j: y_copy(t, j).wait_recv())
         each(1, 8, lambda j: y_relay(t, j).wait_recv())
 
+    big = 4 * places
+    zero = jnp.zeros((places, 128), F32)
+    ones = jnp.where(lanes == HEAD, 1.0, zero)
+
+    def rows_of(block):
+        return pl.ds(pl.multiple_of(block * places, places), places)
+
+    def spread_first(block):
+        rows = rows_of(block)
+        one = fa[block, 0:places].astype(F32)
+        two = fa[block, places : 2 * places].astype(F32)
+        qs[0, rows, :] = fa[block, 0:places]
+        ks[0, rows, :] = jnp.where(
+            lanes < 56, roll_lanes(one, -72), jnp.where(lanes < HEAD, roll_lanes(two, 56), zero)
+        ).astype(BF)
+        vs[0, rows, :] = jnp.where(lanes < HEAD, roll_lanes(two, -16), ones).astype(BF)
+
+    def spread_second(block):
+        rows = rows_of(block)
+        two = fa[block, places : 2 * places].astype(F32)
+        three = fb[block, 0:places].astype(F32)
+        packed = fb[block, places : places + half].astype(F32)
+        left = jnp.concatenate([packed, roll_lanes(packed, 64)], axis=0)
+        qs[1, rows, :] = jnp.where(lanes < 40, roll_lanes(two, -88), roll_lanes(three, 40)).astype(BF)
+        ks[1, rows, :] = jnp.where(lanes < HEAD, roll_lanes(three, -32), zero).astype(BF)
+        vs[1, rows, :] = jnp.where(
+            lanes < 24, roll_lanes(three, -104), jnp.where(lanes < HEAD, roll_lanes(left, 24), ones)
+        ).astype(BF)
+
+    lanes40 = lane_iota(40)
+    lanes16 = lane_iota(16)
+
+    def attend(head, first):
+        rows = pl.ds(pl.multiple_of(first * places, places), big)
+        scores = lax.dot_general(
+            qs[head, rows, :], ks[head], (((1,), (1,)), ((), ())), preferred_element_type=F32
+        )
+        largest = jnp.max(scores, axis=1, keepdims=True)
+        weights = jnp.exp2((scores - largest) * EXP2_SCALE).astype(BF)
+        product = jnp.dot(weights, vs[head], preferred_element_type=F32)
+        mixed = product * (1.0 / product[:, HEAD : HEAD + 1])
+        for part in range(4):
+            val = mixed[part * places : (part + 1) * places]
+            top = jnp.where(lanes40 < HEAD, val[0:40], roll_lanes(val[56:96], 72))
+            last = jnp.concatenate([val[88:96], val[88:96]], axis=0)
+            low = jnp.where(
+                lanes16 < HEAD,
+                val[40:56],
+                jnp.where(
+                    lanes16 < 88,
+                    roll_lanes(val[56:72], 16),
+                    jnp.where(lanes16 < 104, roll_lanes(val[72:88], 32), roll_lanes(last, 48)),
+                ),
+            )
+            ob[head, first + part, 0:40] = top.astype(BF)
+            ob[head, first + part, 40:56] = low.astype(BF)
+
+    def z_back(head, target):
+        return send(
+            ob.at[head, far * 8 + target], zro.at[head, target], zos.at[head, target],
+            zor.at[head, target], partner,
+        )
+
+    def z_back_home(head):
+        return send(
+            ob.at[head, far * 8 + y], mixb.at[1, head, y], zos.at[head, y], zor.at[head, y], partner
+        )
+
+    def y_back(head, j):
+        target = lax.rem(y + j, 8)
+        return send(
+            ob.at[head, a * 8 + target], mixb.at[0, head, y], yos.at[head, 0, j],
+            yor.at[head, 0, j], (f, a * 8 + target),
+        )
+
+    def y_back_relay(head, target):
+        j = lax.rem(target + 8 - y, 8)
+        return send(
+            zro.at[head, target], mixb.at[1, head, y], yos.at[head, 1, j], yor.at[head, 1, j],
+            (f, a * 8 + target),
+        )
+
+    def y_back_arrival(head, which, j):
+        source = lax.rem(y + 8 - j, 8)
+        return send(
+            zro.at[head, 0], mixb.at[which, head, source], yos.at[head, which, j],
+            yor.at[head, which, j], (f, a * 8 + lax.rem(y + j, 8)),
+        )
+
+    def attend_all(head):
+        def z_back_start(target):
+            @pl.when(target != y)
+            def _():
+                z_back(head, target).start()
+
+            @pl.when(target == y)
+            def _():
+                z_back_home(head).start()
+
+        def far_part(step):
+            attend(head, far * 8 + 4 * step)
+            each(4 * step, 4 * step + 4, z_back_start)
+
+        each(0, 2, far_part)
+        each(0, 2, lambda step: attend(head, a * 8 + 4 * step))
+        each(1, 8, lambda j: y_back(head, j).start())
+        mixb[0, head, y] = ob[head, s]
+
+    def relay_back(head):
+        def one(target):
+            @pl.when(target != y)
+            def _():
+                z_back(head, target).wait_recv()
+                y_back_relay(head, target).start()
+
+        each(0, 8, one)
+
     each(1, 8, lambda j: forward(0, j))
+    settle(0)
+    each(0, 16, spread_first)
+    attend_all(0)
     each(1, 8, lambda j: forward(1, j))
-    settle(0)
     settle(1)
-
-    zero = jnp.zeros((places, 128), F32)
-
-    def spread(block):
-        rows = pl.ds(pl.multiple_of(block * places, places), places)
-        main = fk[block, 0:places].astype(F32)
-        packed = fk[block, places : places + half].astype(F32)
-        left = jnp.concatenate([packed, roll_lanes(packed, 64)], axis=0)
-        k0[rows, :] = jnp.where(lanes < HEAD, main, zero).astype(BF)
-        k1[rows, 0:128] = jnp.where(lanes < HEAD, zero, main).astype(BF)
-        k1[rows, 128:256] = jnp.where(lanes < 16, left, zero).astype(BF)
-        qs[rows, 0:128] = fq[block]
-        qs[rows, 128:256] = roll_lanes(left, -16).astype(BF)
-        vs[rows, 128:256] = jnp.where(
-            lanes < 16, roll_lanes(left, -32), jnp.where(lanes == 16, 1.0, 0.0)
-        ).astype(BF)
-
-    each(0, 16, spread)
-
-    big = 4 * places
-
-    def weigh(step):
-        rows = pl.ds(pl.multiple_of(step * big, big), big)
-        for head in range(2):
-            if head == 0:
-                left_side, keys = qs[rows, 0:128], k0[...]
-            else:
-                left_side, keys = qs[rows, :], k1[...]
-            scores = lax.dot_general(
-                left_side, keys, (((1,), (1,)), ((), ())), preferred_element_type=F32
-            )
-            largest = jnp.max(scores, axis=1, keepdims=True)
-            pr[head, rows, :] = jnp.exp2((scores - largest) * EXP2_SCALE).astype(BF)
-        forward(2, 2 * step + 1)
-
-        @pl.when(step < 3)
-        def _():
-            forward(2, 2 * step + 2)
-
-    each(0, 4, weigh)
-    settle(2)
-
-    def place_v(block):
-        rows = pl.ds(pl.multiple_of(block * places, places), places)
-        vs[rows, 0:128] = fv[block]
-
-    each(0, 16, place_v)
-
-    sub_lanes = lane_iota(16)
-
-    def mix(first):
-        rows = pl.ds(pl.multiple_of(first * places, places), big)
-        mixed = []
-        for head in range(2):
-            product = jnp.dot(pr[head, rows, :], vs[...], preferred_element_type=F32)
-            inverse = 1.0 / product[:, 144:145]
-            mixed.append(product * inverse)
-        for part in range(4):
-            cut = slice(part * places, (part + 1) * places)
-            ob[first + part, 0:places] = jnp.where(
-                lanes < HEAD, mixed[0][cut, 0:128], mixed[1][cut, 0:128]
-            ).astype(BF)
-            rest = mixed[1][cut, 128:256]
-            packed = rest[0:16]
-            for group in range(1, 6):
-                moved = roll_lanes(rest[16 * group : 16 * group + 16], 16 * group)
-                packed = jnp.where(sub_lanes < 16 * group, packed, moved)
-            ob[first + part, places : places + 16] = packed.astype(BF)
-
-    def z_back(target):
-        return send(
-            ob.at[far * 8 + target], zro.at[target], zos.at[target], zor.at[target], partner
-        )
-
-    def z_back_home():
-        return send(ob.at[far * 8 + y], mixb.at[1, y], zos.at[y], zor.at[y], partner)
-
-    def y_back(j):
-        target = lax.rem(y + j, 8)
-        return send(
-            ob.at[a * 8 + target], mixb.at[0, y], yos.at[0, j], yor.at[0, j],
-            (f, a * 8 + target),
-        )
-
-    def y_back_relay(target):
-        j = lax.rem(target + 8 - y, 8)
-        return send(
-            zro.at[target], mixb.at[1, y], yos.at[1, j], yor.at[1, j], (f, a * 8 + target)
-        )
-
-    def z_back_start(target):
-        @pl.when(target != y)
-        def _():
-            z_back(target).start()
-
-        @pl.when(target == y)
-        def _():
-            z_back_home().start()
-
-    def far_part(step):
-        mix(far * 8 + 4 * step)
-        each(4 * step, 4 * step + 4, z_back_start)
-
-    def near_part(step):
-        mix(a * 8 + 4 * step)
-
-    each(0, 2, far_part)
-    each(0, 2, near_part)
-    each(1, 8, lambda j: y_back(j).start())
-    mixb[0, y] = ob[s]
-
+    each(0, 16, spread_second)
+    attend_all(1)
+    relay_back(0)
     for load in loads[3:]:
         load.wait()
 
     def project(kind, frame):
-        packs = [mixb[kind, pair, places : places + 16].astype(F32) for pair in range(8)]
         for pair in range(8):
-            am[kind, :, 128 * pair : 128 * pair + 128] = mixb[kind, pair, 0:places]
-        for group in range(6):
-            joined = roll_lanes(packs[0], -16 * group)
-            for pair in range(1, 8):
-                moved = roll_lanes(packs[pair], 16 * pair - 16 * group)
-                joined = jnp.where(sub_lanes < 16 * pair, joined, moved)
-            am[kind, 16 * group : 16 * group + 16, 1024:1152] = joined.astype(BF)
+            for head in range(2):
+                spot = slice(256 * pair + 128 * head, 256 * pair + 128 * head + 128)
+                block = mixb[kind, head, pair].astype(F32)
+                tail = block[40:56]
+                low = jnp.concatenate(
+                    [roll_lanes(tail, -16), roll_lanes(tail, -32), roll_lanes(tail[0:8], -48)],
+                    axis=0,
+                )
+                am[kind, 0:56, spot] = mixb[kind, head, pair]
+                am[kind, 56:96, spot] = jnp.where(
+                    lanes40 < 56, roll_lanes(block[0:40], -72), low
+                ).astype(BF)
         branch = jnp.dot(am[kind], wp[...], preferred_element_type=F32)
         res = (res_ref[frame].astype(F32) + mod_ref[2:3, :] * branch).astype(BF)
         res_out[frame] = res
@@ -403,31 +422,17 @@
         each(1, 8, lambda i: row_copy(kind, level, i, False).start())
         rb[kind, 8 * level + kme] = zx[kind, level, kme]
 
-    each(1, 8, lambda j: y_back(j).wait_recv())
+    for head in range(2):
+        each(1, 8, lambda j: y_back_arrival(head, 0, j).wait_recv())
     width = wt.shape[0]
     inner = width // 3
     pf[:, 1664:1792] = jnp.zeros((2 * places, 128), F32)
     project(0, a)
     exchange(0)
-    def relay_back(target):
-        @pl.when(target != y)
-        def _():
-            z_back(target).wait_recv()
-            y_back_relay(target).start()
-
-    each(0, 8, relay_back)
-    z_back_home().wait_recv()
-
-    def relay_end(j):
-        copy = send(
-            zro.at[0], mixb.at[1, 0], yos.at[1, j], yor.at[1, j], (f, a * 8 + lax.rem(y + j, 8))
-        )
-        copy.wait_recv()
-        copy.wait_send()
-
-    each(1, 8, relay_end)
-    each(1, 8, lambda j: y_back(j).wait_send())
-
+    relay_back(1)
+    for head in range(2):
+        z_back_home(head).wait_recv()
+        each(1, 8, lambda j: y_back_arrival(head, 1, j).wait_recv())
     project(1, far)
     exchange(1)
     for kind in range(2):
@@ -549,8 +554,11 @@
         each(1, 8, one)
 
     each(0, 6, drain)
-    each(0, 8, lambda target: z_back(target).wait_send())
-    for t in range(3):
+    for head in range(2):
+        each(0, 8, lambda target: z_back(head, target).wait_send())
+        for which in range(2):
+            each(1, 8, lambda j: y_back_arrival(head, which, j).wait_send())
+    for t in range(2):
         z_home(t).wait_send()
         each(1, 8, lambda j: z_copy(t, j).wait_send())
         each(1, 8, lambda j: y_copy(t, j).wait_send())
@@ -579,26 +587,21 @@
             pltpu.VMEM(local, BF),
             pltpu.VMEM(local, BF),
             pltpu.VMEM(local, BF),
-            pltpu.VMEM((features, features), BF),
+            pltpu.VMEM((16 * 128, features), BF),
             pltpu.VMEM((width, features), BF),
+            pltpu.VMEM((2, 8, 2 * places, 128), BF),
             pltpu.VMEM((2, 8, places + half, 128), BF),
-            pltpu.VMEM((2, 8, places, 128), BF),
-            pltpu.VMEM((2, 8, places, 128), BF),
+            pltpu.VMEM((8, 2 * places, 128), BF),
             pltpu.VMEM((8, places + half, 128), BF),
-            pltpu.VMEM((8, places, 128), BF),
-            pltpu.VMEM((8, places, 128), BF),
+            pltpu.VMEM((16, 2 * places, 128), BF),
             pltpu.VMEM((16, places + half, 128), BF),
-            pltpu.VMEM((16, places, 128), BF),
-            pltpu.VMEM((16, places, 128), BF),
-            pltpu.VMEM((total, 256), BF),
-            pltpu.VMEM((total, 128), BF),
-            pltpu.VMEM((total, 256), BF),
-            pltpu.VMEM((total, 256), BF),
-            pltpu.VMEM((2, total, total), BF),
-            pltpu.VMEM((16, places + 16, 128), BF),
-            pltpu.VMEM((8, places + 16, 128), BF),
-            pltpu.VMEM((2, 8, places + 16, 128), BF),
-            pltpu.VMEM((2, places, features), BF),
+            pltpu.VMEM((2, total, 128), BF),
+            pltpu.VMEM((2, total, 128), BF),
+            pltpu.VMEM((2, total, 128), BF),
+            pltpu.VMEM((2, 16, 56, 128), BF),
+            pltpu.VMEM((2, 8, 56, 128), BF),
+            pltpu.VMEM((2, 2, 8, 56, 128), BF),
+            pltpu.VMEM((2, places, 16 * 128), BF),
             pltpu.VMEM((2 * places, 1792), F32),
             pltpu.VMEM((2, 48, 2, 1792), BF),
             pltpu.VMEM((2, 6, 8, 2, 1792), BF),
@@ -608,13 +611,13 @@
             pltpu.VMEM((6, 8, 4, 640), BF),
             pltpu.VMEM((48, 4, 640), BF),
             dma((21,)),
-            dma((3, 8)), dma((3, 8)), dma((2, 3, 8)), dma((2, 3, 8)),
-            dma((8,)), dma((8,)), dma((2, 8)), dma((2, 8)),
+            dma((2, 8)), dma((2, 8)), dma((2, 2, 8)), dma((2, 2, 8)),
+            dma((2, 8)), dma((2, 8)), dma((2, 2, 8)), dma((2, 2, 8)),
             dma((2, 6)), dma((2, 6)), dma((2, 6, 8)), dma((2, 6, 8)),
             dma((6,)), dma((6,)), dma((6, 8)), dma((6, 8)),
         ],
         compiler_params=pltpu.CompilerParams(
-            collective_id=1, has_side_effects=True, vmem_limit_bytes=52 << 20
+            collective_id=1, has_side_effects=True, vmem_limit_bytes=67043328
         ),
         name="block",
     )(residual_in, q_spatial, k_spatial, v_spatial, w_out, modulation, w_temporal.T)

time: 146 us -> 161 us (1.10)
  the two profiles are of different devices: /device:TPU:57 before, /device:TPU:1 now
where the time goes in v3:
time: 161 us; the launch traced here: 160 us
  Pallas kernels  156 us (97%)
  local copies, waits for them, and re-layouts  3.47 us (2%)
    pallas_call x1, Pallas kernels, per_device(): pl.pallas_call(block_kernel, out_shape=(jax.ShapeDtypeStruct(local, BF),...  156 us
    unnamed x2, local copies, waits for them, and re-layouts  3.47 us

profile of v3, /device:TPU:1, one launch (start us, length us, event | category | flops | bytes accessed | tf_op | source)
XLA Modules:
  0.0 160.4 jit_solution(720608117566147859)
XLA Ops:
  0.6 156.3 %block.1 = (bf16[2,96,1152]{2,1,0:T(8,128)(2,1)}, bf16[2,96,576]{2,1,0:T(8,128)(2,1)}) custom-call(bf16[2,96,1152]{2,1,0:T(8,128)(2,1)} %res_hbm.1, bf16[2,96,1152]{2,1,0:T(8,128)(2,1)} %q_hbm.1, bf16[2,96,1152]{2,1,0:T(8,128)(2,1)} %k_hbm.1, bf16[2,96,1152]{2,1,0:T(8,128)(2,1)} %v_hbm.1, bf16[1152,1152]{1,0:T(8,128)(2,1)} %wo_hbm.1, f32[3,1152]{1,0:T(4,128)} %mod_ref.1, ...), custom_call_target="tpu_custom_call" | custom-call | tf_op jit(solution)/shard_map/block/pallas_call | solution.py:577
  157.0 1.8 %copy.11 = bf16[2,96,1152]{2,1,0:T(8,128)(2,1)} copy(bf16[2,96,1152]{2,1,0:T(8,128)(2,1)} %get-tuple-element.4) | data formatting | bytes 884736
  158.8 1.7 %copy.12 = bf16[2,96,576]{2,1,0:T(8,128)(2,1)} copy(bf16[2,96,576]{2,1,0:T(8,128)(2,1)} %get-tuple-element.5) | data formatting | bytes 442368

commit v4 on v2

--- a/solution.py
+++ b/solution.py
@@ -13,7 +13,7 @@
 T_HEADS = 8
 BF = jnp.bfloat16
 F32 = jnp.float32
-ORDER = (3, 2, 4, 1, 5)
+ORDER = (1, 2, 3, 4, 5)
 EXP2_SCALE = math.log2(math.e) / math.sqrt(HEAD)
 
 
@@ -219,7 +219,6 @@
     each(1, 8, lambda j: forward(0, j))
     each(1, 8, lambda j: forward(1, j))
     settle(0)
-    settle(1)
 
     zero = jnp.zeros((places, 128), F32)
 
@@ -231,13 +230,19 @@
         k0[rows, :] = jnp.where(lanes < HEAD, main, zero).astype(BF)
         k1[rows, 0:128] = jnp.where(lanes < HEAD, zero, main).astype(BF)
         k1[rows, 128:256] = jnp.where(lanes < 16, left, zero).astype(BF)
-        qs[rows, 0:128] = fq[block]
         qs[rows, 128:256] = roll_lanes(left, -16).astype(BF)
         vs[rows, 128:256] = jnp.where(
             lanes < 16, roll_lanes(left, -32), jnp.where(lanes == 16, 1.0, 0.0)
         ).astype(BF)
 
     each(0, 16, spread)
+    settle(1)
+
+    def place_q(block):
+        rows = pl.ds(pl.multiple_of(block * places, places), places)
+        qs[rows, 0:128] = fq[block]
+
+    each(0, 16, place_q)
 
     big = 4 * places
 
@@ -253,7 +258,8 @@
             )
             largest = jnp.max(scores, axis=1, keepdims=True)
             pr[head, rows, :] = jnp.exp2((scores - largest) * EXP2_SCALE).astype(BF)
-        forward(2, 2 * step + 1)
+            if head == 0:
+                forward(2, 2 * step + 1)
 
         @pl.when(step < 3)
         def _():
@@ -430,9 +436,12 @@
 
     project(1, far)
     exchange(1)
+    for j in ORDER:
+        relay_level(0, 6 - j)
     for kind in range(2):
         for j in ORDER:
-            relay_level(kind, 6 - j)
+            if kind == 1:
+                relay_level(kind, 6 - j)
 
     def gather(kind, level):
         each(1, 8, lambda j: row_arrival(kind, level, j).wait_recv())
@@ -614,7 +623,7 @@
             dma((6,)), dma((6,)), dma((6, 8)), dma((6, 8)),
         ],
         compiler_params=pltpu.CompilerParams(
-            collective_id=1, has_side_effects=True, vmem_limit_bytes=52 << 20
+            collective_id=1, has_side_effects=True, vmem_limit_bytes=67043328
         ),
         name="block",
     )(residual_in, q_spatial, k_spatial, v_spatial, w_out, modulation, w_temporal.T)

time: 146 us -> 140 us (0.959)
  the two profiles are of different devices: /device:TPU:57 before, /device:TPU:1 now
where the time goes in v4:
time: 140 us; the launch traced here: 139 us
  Pallas kernels  135 us (96%)
  local copies, waits for them, and re-layouts  3.47 us (2%)
    pallas_call x1, Pallas kernels, per_device(): pl.pallas_call(block_kernel, out_shape=(jax.ShapeDtypeStruct(local, BF),...  135 us
    unnamed x2, local copies, waits for them, and re-layouts  3.47 us

profile of v4, /device:TPU:1, one launch (start us, length us, event | category | flops | bytes accessed | tf_op | source)
XLA Modules:
  0.0 139.4 jit_solution(18311354462055997928)
XLA Ops:
  0.6 135.3 %block.1 = (bf16[2,96,1152]{2,1,0:T(8,128)(2,1)}, bf16[2,96,576]{2,1,0:T(8,128)(2,1)}) custom-call(bf16[2,96,1152]{2,1,0:T(8,128)(2,1)} %res_hbm.1, bf16[2,96,1152]{2,1,0:T(8,128)(2,1)} %q_hbm.1, bf16[2,96,1152]{2,1,0:T(8,128)(2,1)} %k_hbm.1, bf16[2,96,1152]{2,1,0:T(8,128)(2,1)} %v_hbm.1, bf16[1152,1152]{1,0:T(8,128)(2,1)} %wo_hbm.1, f32[3,1152]{1,0:T(4,128)} %mod_ref.1, ...), custom_call_target="tpu_custom_call" | custom-call | tf_op jit(solution)/shard_map/block/pallas_call | solution.py:578
  135.9 1.8 %copy.11 = bf16[2,96,1152]{2,1,0:T(8,128)(2,1)} copy(bf16[2,96,1152]{2,1,0:T(8,128)(2,1)} %get-tuple-element.4) | data formatting | bytes 884736
  137.7 1.7 %copy.12 = bf16[2,96,576]{2,1,0:T(8,128)(2,1)} copy(bf16[2,96,576]{2,1,0:T(8,128)(2,1)} %get-tuple-element.5) | data formatting | bytes 442368
